TPU v7x, 32 devices: a whole 2x2x4 slice. The times are simulated.
32 devices in a mesh: fsdp: 4 (over y, core), ctx: 2 (over x), tp: 4 (over z).
Axes of the slice: x: 2, y: 2, z: 4, core: 2. Of those that a mesh axis runs over, the one named last changes fastest.
Arguments:
- tokens: bfloat16 [8, 1024, 1024], P('fsdp', 'ctx'), may hold values from -16 to 16
- gain1: bfloat16 [1024], P('fsdp'), may hold values from 0.5 to 1.5
- w_latent: bfloat16 [1024, 512], P('fsdp'), may hold values from -0.1875 to 0.1875
- w_query: bfloat16 [1024, 1024], P('fsdp', 'tp'), may hold values from -0.1875 to 0.1875
- w_key: bfloat16 [256, 1024], P('fsdp', 'tp'), may hold values from -0.375 to 0.375
- w_value: bfloat16 [256, 1024], P('fsdp', 'tp'), may hold values from -0.375 to 0.375
- w_out: bfloat16 [1024, 1024], P('tp', 'fsdp'), may hold values from -1.5 to 1.5
- gain2: bfloat16 [1024], P('fsdp'), may hold values from 0.5 to 1.5
- w_gate: bfloat16 [1024, 2816], P('fsdp', 'tp'), may hold values from -0.1875 to 0.1875
- w_up: bfloat16 [1024, 2816], P('fsdp', 'tp'), may hold values from -0.1875 to 0.1875
- w_down: bfloat16 [2816, 1024], P('tp', 'fsdp'), may hold values from -0.109375 to 0.109375
- segments: int32 [8, 1024], P('fsdp', 'ctx'), may hold values from 0 to 7, never falling along the last dimension, each value on 1 to 512 neighbouring positions
- cotangent: bfloat16 [8, 1024, 1024], P('fsdp', 'ctx'), may hold values from -6 to 6
Outputs:
- mixed: bfloat16 [8, 1024, 1024], P('fsdp', 'ctx')
- grad_tokens: bfloat16 [8, 1024, 1024], P('fsdp', 'ctx')
- grad_gain1: float32 [1024], P('fsdp')
- grad_latent: float32 [1024, 512], P('fsdp')
- grad_query: float32 [1024, 1024], P('fsdp', 'tp')
- grad_key: float32 [256, 1024], P('fsdp', 'tp')
- grad_value: float32 [256, 1024], P('fsdp', 'tp')
- grad_out: float32 [1024, 1024], P('tp', 'fsdp')
- grad_gain2: float32 [1024], P('fsdp')
- grad_gate: float32 [1024, 2816], P('fsdp', 'tp')
- grad_up: float32 [1024, 2816], P('fsdp', 'tp')
- grad_down: float32 [2816, 1024], P('tp', 'fsdp')
- stats: float32 [8, 3], P('fsdp')
- grad_radial: float32 [8, 1024], P('fsdp', 'ctx')
Inputs may be any that keep to these rules, and one draw needn't show every extreme that they name: `segments`: ids never fall along a sequence; every id of 0 to 7 names 1 to 512 consecutive tokens of each sequence, and some id names exactly 512; the largest id of a sequence marks its padding.
All inputs are finite; a program needn't handle non-finite values.
Results may differ from a plain program's by a relative error of at most 0.013.
The roundings to bfloat16 on the way count: a program that leaves them out, or rounds other values in their place, can miss the bound.
Values may be sent and summed in bfloat16 or wider, within the bound.
A program may use at most 128 MiB of HBM per device.

v0:
```python
import jax
import jax.numpy as jnp
from jax import lax
from jax.experimental import pallas as pl
from jax.experimental.pallas import tpu as pltpu
from jax.sharding import PartitionSpec as P

HEADS = 16
HEAD_DIM = 64
GROUPS = 2
LATENT = 256
MESH = pl.DeviceIdType.MESH
VMEM = pl.BlockSpec(memory_space=pltpu.VMEM)
ANY = pl.BlockSpec(memory_space=pl.ANY)
F32 = jnp.float32
BF16 = jnp.bfloat16

eps = 1e-05


def remote(src, dst, send_sem, recv_sem, device):
    return pltpu.make_async_remote_copy(
        src_ref=src,
        dst_ref=dst,
        send_sem=send_sem,
        recv_sem=recv_sem,
        device_id=device,
        device_id_type=MESH,
    )


def wait_sent(ref, sem, recv_sem):
    remote(ref, ref, sem, recv_sem, {"tp": lax.axis_index("tp")}).wait_send()


def wait_came(ref, send_sem, sem):
    remote(ref, ref, send_sem, sem, {"tp": lax.axis_index("tp")}).wait_recv()


def meet(line=0, fsdp=0, ctx=0, everyone=False):
    barrier = pltpu.get_barrier_semaphore()

    def greet(device):
        pl.semaphore_signal(barrier, inc=1, device_id=device, device_id_type=MESH)

    known = 0
    f, x, me = lax.axis_index("fsdp"), lax.axis_index("ctx"), lax.axis_index("tp")
    if fsdp and everyone:
        for k in range(1, fsdp):
            greet({"fsdp": lax.rem(f + k, fsdp)})
        known += fsdp - 1
    elif fsdp:
        greet({"fsdp": sibling(f)})
        for k in range(1, fsdp // 2):
            greet({"fsdp": lax.rem(f + 2 * k, fsdp)})
        known += fsdp // 2
    for k in range(1, ctx):
        greet({"ctx": lax.rem(x + k, ctx)})
        known += 1
    if line > 1 and everyone:
        for k in range(1, line):
            greet({"tp": lax.rem(me + k, line)})
        known += line - 1
    if line > 1 and not everyone:

        @pl.when(me > 0)
        def _():
            greet({"tp": me - 1})

        @pl.when(me < line - 1)
        def _():
            greet({"tp": me + 1})

        @pl.when((me > 0) & (me < line - 1))
        def _():
            pl.semaphore_wait(barrier, known + 2)

        @pl.when((me == 0) | (me == line - 1))
        def _():
            pl.semaphore_wait(barrier, known + 1)

    else:
        pl.semaphore_wait(barrier, known)


def sibling(f):
    return f + 1 - 2 * lax.rem(f, 2)


def block(ref, axis, index, size):
    at = pl.ds(pl.multiple_of(index * size, size), size)
    return ref.at[at] if axis == 0 else ref.at[:, at]


class Bring:
    def __init__(self, pairs, sems):
        self.copies = [pltpu.make_async_copy(src, dst, sems.at[i]) for i, (src, dst) in enumerate(pairs)]

    def start(self, which=None):
        for i in which if which is not None else range(len(self.copies)):
            self.copies[i].start()

    def wait(self, which=None):
        for i in which if which is not None else range(len(self.copies)):
            self.copies[i].wait()


class Spread:
    def __init__(self, fsdp, pairs, axes, recv, sent, own):
        self.fsdp, self.pairs, self.axes = fsdp, pairs, axes
        self.recv, self.sent, self.own = recv, sent, own
        self.f = lax.axis_index("fsdp")

    def size(self, a):
        return self.pairs[a][0].shape[self.axes[a]]

    def target(self, a, f):
        return block(self.pairs[a][1], self.axes[a], f, self.size(a))

    def start(self):
        f = self.f
        for a, (src, dst) in enumerate(self.pairs):
            for k in range(1, self.fsdp // 2):
                remote(src, self.target(a, f), self.sent.at[a], self.recv.at[a, f],
                       {"fsdp": lax.rem(f + 2 * k, self.fsdp)}).start()
        for a, (src, dst) in enumerate(self.pairs):
            remote(src, self.target(a, f), self.sent.at[a], self.recv.at[a, f],
                   {"fsdp": sibling(f)}).start()
            pltpu.make_async_copy(src, self.target(a, f), self.own.at[a]).start()

    def relay(self, which=None):
        for a in which or range(len(self.pairs)):
            for k in range(1, self.fsdp // 2):
                other = lax.rem(self.f + 2 * k, self.fsdp)
                here = self.target(a, other)
                wait_came(here, self.sent.at[a], self.recv.at[a, other])
                remote(here, here, self.sent.at[a], self.recv.at[a, other],
                       {"fsdp": sibling(self.f)}).start()

    def finish(self, which=None):
        for a in which or range(len(self.pairs)):
            src, dst = self.pairs[a]
            for k in range(0, self.fsdp // 2):
                other = lax.rem(sibling(self.f) + 2 * k, self.fsdp)
                wait_came(self.target(a, other), self.sent.at[a], self.recv.at[a, other])
            pltpu.make_async_copy(src, self.target(a, self.f), self.own.at[a]).wait()
            many = (self.fsdp - 1) * self.size(a)
            ref = dst.at[pl.ds(0, many)] if self.axes[a] == 0 else dst.at[:, pl.ds(0, many)]
            wait_sent(ref, self.sent.at[a], self.recv.at[a, 0])

    @staticmethod
    def scratch(fsdp, arrays):
        return [
            pltpu.SemaphoreType.DMA((arrays, fsdp)),
            pltpu.SemaphoreType.DMA((arrays,)),
            pltpu.SemaphoreType.DMA((arrays,)),
        ]


class CtxShare:
    def __init__(self, ctx, src, dst, recv, sent, own):
        self.ctx, self.src, self.dst = ctx, src, dst
        self.recv, self.sent, self.own = recv, sent, own
        self.x = lax.axis_index("ctx")

    def start(self):
        for k in range(1, self.ctx):
            remote(self.src, self.dst.at[self.x], self.sent.at[k - 1], self.recv.at[self.x],
                   {"ctx": lax.rem(self.x + k, self.ctx)}).start()
        pltpu.make_async_copy(self.src, self.dst.at[self.x], self.own).start()

    def finish(self):
        for k in range(1, self.ctx):
            other = lax.rem(self.x + k, self.ctx)
            wait_came(self.dst.at[other], self.sent.at[k - 1], self.recv.at[other])
            wait_sent(self.src, self.sent.at[k - 1], self.recv.at[other])
        pltpu.make_async_copy(self.src, self.dst.at[self.x], self.own).wait()

    @staticmethod
    def scratch(ctx):
        return [
            pltpu.SemaphoreType.DMA((ctx,)),
            pltpu.SemaphoreType.DMA((ctx,)),
            pltpu.SemaphoreType.DMA,
        ]


class LineGather:
    def __init__(self, n, chunk, src, dst, recv, sent, own):
        self.n, self.chunk, self.src, self.dst = n, chunk, src, dst
        self.width = src.shape[1]
        self.count = src.shape[0] // chunk
        self.recv, self.sent, self.own = recv, sent, own
        self.me = lax.axis_index("tp")

    def steps(self):
        return self.count + self.n - 1

    def columns(self, tp):
        return pl.ds(pl.multiple_of(tp * self.width, self.width), self.width)

    def place(self, tp, at):
        rows = pl.ds(pl.multiple_of(at * self.chunk, self.chunk), self.chunk)
        return self.dst.at[rows, self.columns(tp)]

    def begin(self):
        pltpu.make_async_copy(self.src, self.dst.at[:, self.columns(self.me)], self.own).start()

    def begun(self):
        pltpu.make_async_copy(self.src, self.dst.at[:, self.columns(self.me)], self.own).wait()

    def step(self, s):
        n, me, count = self.n, self.me, self.count
        left, right = {"tp": me - 1}, {"tp": me + 1}

        @pl.when((s >= 0) & (s < count))
        def _():
            rows = pl.ds(pl.multiple_of(s * self.chunk, self.chunk), self.chunk)

            @pl.when(me > 0)
            def _():
                remote(self.src.at[rows], self.place(me, s), self.sent.at[0], self.recv.at[me, s], left).start()

            @pl.when(me < n - 1)
            def _():
                remote(self.src.at[rows], self.place(me, s), self.sent.at[1], self.recv.at[me, s], right).start()

        for away in range(1, n):
            at = s - away
            for sign, onward in ((-1, right), (1, left)):
                tp = me + sign * away

                @pl.when((tp >= 0) & (tp < n) & (at >= 0) & (at < count))
                def _(tp=tp, onward=onward, sign=sign, at=at):
                    here = self.place(tp, at)
                    wait_came(here, self.sent.at[2], self.recv.at[tp, at])

                    @pl.when((me < n - 1) if sign < 0 else (me > 0))
                    def _():
                        remote(here, here, self.sent.at[2], self.recv.at[tp, at], onward).start()

    def drain(self):
        n, me = self.n, self.me

        @pl.when(me > 0)
        def _():
            wait_sent(self.src, self.sent.at[0], self.recv.at[0, 0])

        @pl.when(me < n - 1)
        def _():
            wait_sent(self.src, self.sent.at[1], self.recv.at[0, 0])

        @pl.when((me > 0) & (me < n - 1))
        def _():
            wait_sent(self.dst.at[:, pl.ds(0, (n - 1) * self.width)], self.sent.at[2], self.recv.at[0, 0])

    @staticmethod
    def scratch(n, count):
        return [
            pltpu.SemaphoreType.DMA((n, count)),
            pltpu.SemaphoreType.DMA((3,)),
            pltpu.SemaphoreType.DMA,
        ]


class LineSum:
    def __init__(self, n, chunk, hop, part, from_left, from_right, out, recv, sent, finish):
        self.n, self.chunk, self.hop = n, chunk, hop
        self.total_rows = part.shape[0]
        self.owners = (n // 2 - 1, n // 2)
        self.count = self.total_rows // 2 // chunk
        self.part, self.from_left, self.from_right, self.out = part, from_left, from_right, out
        self.recv, self.sent = recv, sent
        self.finish = finish
        self.me = lax.axis_index("tp")

    def steps(self):
        return self.count + self.hop * 2 * (self.n // 2)

    def rows(self, slot, at):
        return pl.ds(pl.multiple_of((at * 2 + slot) * self.chunk, self.chunk), self.chunk)

    def step(self, s):
        n, me, hop = self.n, self.me, self.hop
        left, right = {"tp": me - 1}, {"tp": me + 1}
        reach = n // 2
        for slot, owner in enumerate(self.owners):
            for side in (0, 1):
                lag = me if side == 0 else n - 1 - me
                at = s - hop * lag
                here = (me < owner) if side == 0 else (me > owner)
                held = self.from_left if side == 0 else self.from_right
                to = right if side == 0 else left
                here = here & (at >= 0) & (at < self.count)

                @pl.when(here & (lag == 0))
                def _(at=at, held=held, to=to, side=side, slot=slot):
                    rows = self.rows(slot, at)
                    remote(self.part.at[rows], held.at[rows], self.sent.at[0],
                           self.recv.at[side, slot, at], to).start()

                if n > 2:

                    @pl.when(here & (lag > 0))
                    def _(at=at, held=held, to=to, side=side, slot=slot):
                        rows = self.rows(slot, at)
                        wait_came(held.at[rows], self.sent.at[0], self.recv.at[side, slot, at])
                        held[rows, :] = (held[rows, :].astype(F32) + self.part[rows, :].astype(F32)).astype(BF16)
                        remote(held.at[rows], held.at[rows], self.sent.at[0],
                               self.recv.at[side, slot, at], to).start()

            at = s - hop * reach

            @pl.when((me == owner) & (at >= 0) & (at < self.count))
            def _(at=at, slot=slot, owner=owner):
                rows = self.rows(slot, at)
                total = self.part[rows, :].astype(F32)
                if owner > 0:
                    wait_came(self.from_left.at[rows], self.sent.at[0], self.recv.at[0, slot, at])
                    total = total + self.from_left[rows, :].astype(F32)
                wait_came(self.from_right.at[rows], self.sent.at[0], self.recv.at[1, slot, at])
                total = total + self.from_right[rows, :].astype(F32)
                own = pl.ds(pl.multiple_of(at * self.chunk, self.chunk), self.chunk)
                self.out[rows, :] = self.finish(rows, own, total)
                if owner > 0:
                    remote(self.out.at[rows], self.out.at[rows], self.sent.at[1],
                           self.recv.at[2, slot, at], left).start()
                remote(self.out.at[rows], self.out.at[rows], self.sent.at[2],
                       self.recv.at[2, slot, at], right).start()

        for slot, owner in enumerate(self.owners):
            away = jnp.abs(me - owner)
            at = s - hop * (reach + away)

            @pl.when((me != owner) & (at >= 0) & (at < self.count))
            def _(at=at, slot=slot, owner=owner):
                rows = self.rows(slot, at)
                here = self.out.at[rows]
                wait_came(here, self.sent.at[3], self.recv.at[2, slot, at])

                @pl.when((me < owner) & (me > 0))
                def _():
                    remote(here, here, self.sent.at[3], self.recv.at[2, slot, at], left).start()

                @pl.when((me > owner) & (me < n - 1))
                def _():
                    remote(here, here, self.sent.at[3], self.recv.at[2, slot, at], right).start()

    def drain(self):
        n, me, half = self.n, self.me, self.total_rows // 2
        lo, hi = self.owners

        def wait(sem, size):
            wait_sent(self.part.at[pl.ds(0, size)], self.sent.at[sem], self.recv.at[0, 0, 0])

        middle = (me == lo) | (me == hi)

        @pl.when(middle)
        def _():
            wait(0, half)
            wait(2, half)

        @pl.when((me != lo) & (me != hi))
        def _():
            wait(0, 2 * half)

        if lo > 0:

            @pl.when(middle)
            def _():
                wait(1, half)
                wait(3, half)

            if n > 4:

                @pl.when((me != lo) & (me != hi) & (me > 0) & (me < n - 1))
                def _():
                    wait(3, 2 * half)
        else:

            @pl.when(me == hi)
            def _():
                wait(1, half)

    @staticmethod
    def scratch(n, rows, width, chunk):
        return [
            pltpu.VMEM((rows, width), BF16),
            pltpu.VMEM((rows, width), BF16),
            pltpu.SemaphoreType.DMA((3, 2, rows // 2 // chunk)),
            pltpu.SemaphoreType.DMA((4,)),
        ]


class GradSum:
    def __init__(self, fsdp, ctx, parts, axes, outs, held, recv, sent):
        self.fsdp, self.ctx, self.parts, self.axes, self.outs = fsdp, ctx, parts, axes, outs
        self.ys = fsdp // 2
        self.held, self.recv, self.sent = held, recv, sent
        self.f = lax.axis_index("fsdp")
        self.x = lax.axis_index("ctx")
        self.y, self.c = self.f // 2, lax.rem(self.f, 2)

    @staticmethod
    def block_shape(shape, axis, fsdp):
        r, c = shape
        return (r // fsdp, c) if axis == 0 else (r, c // fsdp)

    @staticmethod
    def scratch(fsdp, ctx, shapes, first=True):
        held = []
        for shape in shapes:
            if first:
                held.append(pltpu.VMEM((fsdp // 2,) + shape, BF16))
            held += [
                pltpu.VMEM((max(fsdp // 2 - 1, 1),) + shape, BF16),
                pltpu.VMEM((ctx,) + shape, BF16),
            ]
        return held

    @staticmethod
    def semaphores(fsdp, ctx, count):
        return [pltpu.SemaphoreType.DMA((count, 3, max(fsdp // 2, ctx)))] * 2

    def part(self, a, f):
        shape = self.held[a][0].shape[1:]
        return block(self.parts[a], self.axes[a], f, shape[self.axes[a]])

    def each(self, a, body):
        rows = self.held[a][0].shape[1]
        size = 32 if rows % 32 == 0 else 16

        def step(i, carry):
            body(pl.ds(pl.multiple_of(i * size, size), size))
            return carry

        lax.fori_loop(0, rows // size, step, 0)

    def start(self):
        for a in range(len(self.parts)):
            for k in range(self.ys):
                remote(self.part(a, 2 * k + 1 - self.c), self.held[a][0].at[k], self.sent.at[a, 0, k],
                       self.recv.at[a, 0, k], {"fsdp": sibling(self.f)}).start()

    def pair(self):
        for a in range(len(self.parts)):
            first = self.held[a][0]
            for k in range(self.ys):
                wait_came(first.at[k], self.sent.at[a, 0, k], self.recv.at[a, 0, k])
                mine = self.part(a, 2 * k + self.c)

                def add(rows, first=first, k=k, mine=mine):
                    first[k, rows, :] = (first[k, rows, :].astype(F32) + mine[rows, :].astype(F32)).astype(BF16)

                self.each(a, add)

    def second(self):
        for a in range(len(self.held)):
            first, later = self.held[a][0], self.held[a][1]
            for k in range(1, self.ys):
                to = lax.rem(self.y + k, self.ys)
                remote(first.at[to], later.at[k - 1], self.sent.at[a, 1, k], self.recv.at[a, 1, k],
                       {"fsdp": 2 * to + self.c}).start()

    def third(self):
        for a in range(len(self.held)):
            first, later, last = self.held[a]
            for k in range(1, self.ys):
                wait_came(later.at[k - 1], self.sent.at[a, 1, k], self.recv.at[a, 1, k])

            def add(rows, first=first, later=later, last=last):
                total = first[self.y, rows, :].astype(F32)
                for k in range(1, self.ys):
                    total = total + later[k - 1, rows, :].astype(F32)
                last[self.x, rows, :] = total.astype(BF16)

            self.each(a, add)
            for k in range(1, self.ctx):
                remote(last.at[self.x], last.at[self.x], self.sent.at[a, 2, k], self.recv.at[a, 2, self.x],
                       {"ctx": lax.rem(self.x + k, self.ctx)}).start()

    def fourth(self, store):
        for a in range(len(self.held)):
            last = self.held[a][2]
            for k in range(1, self.ctx):
                other = lax.rem(self.x + k, self.ctx)
                wait_came(last.at[other], self.sent.at[a, 2, k], self.recv.at[a, 2, other])

            def add(rows, last=last, a=a):
                total = last[0, rows, :].astype(F32)
                for k in range(1, self.ctx):
                    total = total + last[k, rows, :].astype(F32)
                store(a, rows, total)

            self.each(a, add)

    def drain_pair(self):
        for a in range(len(self.parts)):
            for k in range(self.ys):
                wait_sent(self.held[a][0].at[k], self.sent.at[a, 0, k], self.recv.at[a, 0, k])

    def drain(self):
        for a in range(len(self.held)):
            first, later, last = self.held[a]
            for k in range(1, self.ys):
                wait_sent(later.at[k - 1], self.sent.at[a, 1, k], self.recv.at[a, 1, k])
            for k in range(1, self.ctx):
                wait_sent(last.at[self.x], self.sent.at[a, 2, k], self.recv.at[a, 2, 0])


def loop(first, last, body):
    def step(s, carry):
        body(s)
        return carry

    lax.fori_loop(first, last, step, 0)


def params(ident, mib):
    return pltpu.CompilerParams(collective_id=ident, has_side_effects=True, vmem_limit_bytes=min(mib << 20, 67043328))


def shape_of(shape, dtype):
    return jax.ShapeDtypeStruct(shape, dtype)


TILE = 256


def dot(left, right):
    return jnp.dot(left, right, preferred_element_type=F32)


def dot_t(left, right):
    return lax.dot_general(left, right, (((1,), (1,)), ((), ())), preferred_element_type=F32)


def dot_rows(left, right):
    return lax.dot_general(left, right, (((0,), (0,)), ((), ())), preferred_element_type=F32)


def head_only(value, head):
    lane = lax.broadcasted_iota(jnp.int32, value.shape, 1)
    return jnp.where((lane // HEAD_DIM) == head, value, jnp.zeros_like(value))


class RowGather:
    def __init__(self, n, src, dst, recv, sent, own):
        self.n, self.src, self.dst = n, src, dst
        self.recv, self.sent, self.own = recv, sent, own
        self.me = lax.axis_index("tp")

    def start(self):
        me = self.me
        pltpu.make_async_copy(self.src, self.dst.at[me], self.own).start()

        @pl.when(me > 0)
        def _():
            remote(self.src, self.dst.at[me], self.sent.at[0, 0], self.recv.at[me], {"tp": me - 1}).start()

        @pl.when(me < self.n - 1)
        def _():
            remote(self.src, self.dst.at[me], self.sent.at[1, 0], self.recv.at[me], {"tp": me + 1}).start()

    def each(self, body, which=None):
        me, n = self.me, self.n
        for away in which or range(1, n):
            for way, tp in ((1, me - away), (0, me + away)):

                @pl.when((tp >= 0) & (tp < n))
                def _(tp=tp, way=way, away=away):
                    onward = (me < n - 1) if way == 1 else (me > 0)
                    body(away, way, tp, onward, {"tp": me + 1} if way == 1 else {"tp": me - 1})

    def relay(self, which=None):
        def body(away, way, tp, onward, to):
            here = self.dst.at[tp]
            wait_came(here, self.sent.at[way, away], self.recv.at[tp])

            @pl.when(onward)
            def _():
                remote(here, here, self.sent.at[way, away], self.recv.at[tp], to).start()

        self.each(body, which)

    def finish(self):
        me = self.me
        pltpu.make_async_copy(self.src, self.dst.at[me], self.own).wait()

        @pl.when(me > 0)
        def _():
            wait_sent(self.src, self.sent.at[0, 0], self.recv.at[0])

        @pl.when(me < self.n - 1)
        def _():
            wait_sent(self.src, self.sent.at[1, 0], self.recv.at[0])

        def body(away, way, tp, onward, to):
            @pl.when(onward)
            def _():
                wait_sent(self.src, self.sent.at[way, away], self.recv.at[0])

        self.each(body)

    @staticmethod
    def scratch(n):
        return [
            pltpu.SemaphoreType.DMA((n,)),
            pltpu.SemaphoreType.DMA((2, n)),
            pltpu.SemaphoreType.DMA,
        ]


class AxisSum:
    def __init__(self, axis, n, slots, recv, sent):
        self.axis, self.n, self.slots, self.recv, self.sent = axis, n, slots, recv, sent
        self.at = lax.axis_index(axis)

    def start(self, value):
        self.slots[self.at] = value
        for k in range(1, self.n):
            remote(self.slots.at[self.at], self.slots.at[self.at], self.sent.at[k], self.recv.at[self.at],
                   {self.axis: lax.rem(self.at + k, self.n)}).start()

    def finish(self):
        for k in range(1, self.n):
            other = lax.rem(self.at + k, self.n)
            wait_came(self.slots.at[other], self.sent.at[k], self.recv.at[other])
            wait_sent(self.slots.at[self.at], self.sent.at[k], self.recv.at[other])
        total = self.slots[0]
        for k in range(1, self.n):
            total = total + self.slots[k]
        return total

    @staticmethod
    def scratch(n, shape):
        return [
            pltpu.VMEM((n,) + shape, F32),
            pltpu.SemaphoreType.DMA((n,)),
            pltpu.SemaphoreType.DMA((n,)),
        ]


def window(ctx, tok_dev):
    return min(ctx, (tok_dev * ctx // 2 + tok_dev - 1) // tok_dev + 1)


def key_span(ctx, tok_dev):
    return min(ctx * tok_dev // 2 // TILE, (window(ctx, tok_dev) - 1) * (tok_dev // TILE))


R_ONE, SEGMENT, VALID = 0, 1, 2


def front(tokens, gain1, gain2, w_latent, shards, w_out, wide_shards, segments, fsdp, ctx, n):
    rows, width = tokens.shape
    seq_dev, tok_dev = segments.shape
    latent, q_width = LATENT, shards[0].shape[1]
    wide, chunk = 128, 256
    pieces = rows // chunk
    win = window(ctx, tok_dev)
    full = [shape_of((s.shape[0] * fsdp,) + s.shape[1:], s.dtype) for s in shards]
    wider = [shape_of((s.shape[0], s.shape[1] * fsdp), s.dtype) for s in wide_shards]
    per_group = HEADS // GROUPS * HEAD_DIM
    per_seq = tok_dev // chunk

    def kernel(*refs):
        (tok_in, ga, gb, wlat, wq, wk, wv, wo, wg, wu, seg), refs = refs[:11], refs[11:]
        (xn_out, cols, gain_all, w_lat, w_qry, w_kproj, w_vproj, gate_all, up_all), refs = refs[:9], refs[9:]
        (wo_all, seg_all, lat_all, query, keys, values), refs = refs[:6], refs[6:]
        (gbuf, sbuf, tok, xn, tsem), refs = refs[:5], refs[5:]
        bring = Bring([(tok_in, tok), (xn, xn_out)], tsem)
        bring.start([0])
        x, me = lax.axis_index("ctx"), lax.axis_index("tp")
        gbuf[...] = jnp.zeros_like(gbuf)
        gbuf[0:1, :] = ga[...].astype(F32).reshape(1, -1)
        gbuf[1:2, :] = gb[...].astype(F32).reshape(1, -1)
        sbuf[...] = jnp.zeros_like(sbuf)
        sbuf[0:seq_dev, :] = seg[...]
        meet(n, fsdp, ctx)
        group = me * q_width // per_group
        src_lat = wlat.at[:, pl.ds(pl.multiple_of(group * latent, latent), latent)]
        pairs = [(gbuf, gain_all), (src_lat, w_lat), (wq, w_qry), (wk, w_kproj), (wv, w_vproj),
                 (wg, gate_all), (wu, up_all)]
        spread = Spread(fsdp, pairs, [1, 0, 0, 0, 0, 1, 1], *refs[:3])
        share = CtxShare(ctx, sbuf, seg_all, *refs[3:6])
        line = RowGather(n, wo, wo_all, *refs[6:9])
        lat_recv, lat_sent = refs[9:11]
        spread.start()
        share.start()
        line.start()
        own = win - 1
        cols[...] = jnp.zeros_like(cols)
        bring.wait([0])

        def scale(i):
            at = pl.ds(pl.multiple_of(i * wide, wide), wide)
            value = tok[at, :].astype(F32)
            cols[at, R_ONE : R_ONE + 1] = lax.rsqrt(jnp.mean(value * value, axis=-1, keepdims=True) + eps)

        loop(0, rows // wide, scale)
        spread.relay([0, 1])
        spread.finish([0, 1])

        def place(shard, i):
            seq = i // per_seq
            return pl.ds(pl.multiple_of(seq * win * tok_dev + shard * tok_dev + lax.rem(i, per_seq) * chunk, chunk), chunk)

        def send(k, i):
            return remote(lat_all.at[place(own, i)], lat_all.at[place(own - k, i)], lat_sent.at[k, i],
                          lat_recv.at[own - k, i], {"ctx": x + k})

        def first(i):
            at = pl.ds(pl.multiple_of(i * chunk, chunk), chunk)
            unit = (tok[at, :].astype(F32) * cols[at, R_ONE : R_ONE + 1] * gain_all[0:1, :]).astype(BF16)
            xn[at, :] = unit
            lat_all[place(own, i), :] = dot(unit, w_lat[...]).astype(BF16)
            for k in range(1, win):

                @pl.when(x + k < ctx)
                def _(k=k):
                    send(k, i).start()

        loop(0, pieces, first)
        bring.start([1])
        line.relay([1])
        spread.relay([2, 3, 4])
        spread.finish([2, 3, 4])

        def project(shard, i):
            to = place(shard, i)
            value = lat_all[to, :]
            keys[to, :] = dot(value, w_kproj[...]).astype(BF16)
            values[to, :] = dot(value, w_vproj[...]).astype(BF16)

        def ask(i):
            at = pl.ds(pl.multiple_of(i * chunk, chunk), chunk)
            query[at, :] = dot(xn[at, :], w_qry[...]).astype(BF16)
            project(own, i)

        loop(0, pieces, ask)
        share.finish()
        for q in range(seq_dev):
            at = slice(q * tok_dev, (q + 1) * tok_dev)
            ids = jnp.broadcast_to(sbuf[q : q + 1, :].astype(F32), (128, tok_dev)).T
            cols[at, SEGMENT : SEGMENT + 1] = ids[:, 0:1]
            last = seg_all[ctx - 1, q : q + 1, tok_dev - 1 : tok_dev].astype(F32)
            cols[at, VALID : VALID + 1] = jnp.where(ids[:, 0:1] != last, 1.0, 0.0)
        line.relay(range(2, n))
        for k in range(1, win):

            def theirs(i, k=k):
                @pl.when(x - k >= 0)
                def _():
                    wait_came(lat_all.at[place(own - k, i)], lat_sent.at[k, i], lat_recv.at[own - k, i])

                @pl.when(x - k < 0)
                def _():
                    lat_all[place(own - k, i), :] = jnp.zeros((chunk, latent), BF16)

                project(own - k, i)

            loop(0, pieces, theirs)

            def gone(i, k=k):
                @pl.when(x + k < ctx)
                def _():
                    send(k, i).wait_send()

            loop(0, pieces, gone)
        spread.relay([5, 6])
        spread.finish([5, 6])
        line.finish()
        bring.wait([1])

    return pl.pallas_call(
        kernel,
        out_shape=(
            shape_of((rows, width), BF16),
            shape_of((rows, 128), F32),
            shape_of((8, width), F32),
            shape_of((width, latent), BF16),
            *full,
            *wider,
            shape_of((n,) + w_out.shape, w_out.dtype),
            shape_of((ctx, 8, tok_dev), segments.dtype),
            shape_of((win * rows, latent), BF16),
            shape_of((rows, q_width), BF16),
            shape_of((win * rows, q_width), BF16),
            shape_of((win * rows, q_width), BF16),
        ),
        in_specs=[ANY] + [VMEM] * 10,
        out_specs=(ANY,) + (VMEM,) * 6 + (ANY,) * 3 + (VMEM,) * 5,
        scratch_shapes=[
            pltpu.VMEM((8, gain1.shape[0]), F32),
            pltpu.VMEM((8, tok_dev), segments.dtype),
            pltpu.VMEM((rows, width), BF16),
            pltpu.VMEM((rows, width), BF16),
            pltpu.SemaphoreType.DMA((2,)),
        ]
        + Spread.scratch(fsdp, 7)
        + CtxShare.scratch(ctx)
        + RowGather.scratch(n)
        + [pltpu.SemaphoreType.DMA((win, pieces))] * 2,
        compiler_params=params(1, 56),
    )(tokens, gain1, gain2, w_latent, *shards, w_out, *wide_shards, segments)


def counted_keys(cols, segk, at, seq, q_first, first, count, tok_dev, win):
    per = tok_dev // TILE
    oldest = lax.axis_index("ctx") - (win - 1)
    mine = cols[at, SEGMENT : SEGMENT + 1]
    shape = (mine.shape[0], TILE)
    pieces = []
    for j in range(count):
        t = first + j
        shard = oldest + t // per
        inner = pl.ds(pl.multiple_of(lax.rem(t, per) * TILE, TILE), TILE)
        ids = segk[jnp.maximum(shard, 0), pl.ds(seq, 1), inner].astype(F32)
        q_at = q_first + lax.broadcasted_iota(jnp.int32, shape, 0)
        k_at = t * TILE + lax.broadcasted_iota(jnp.int32, shape, 1)
        pieces.append((k_at <= q_at) & (ids == mine) & (shard >= 0))
    return pieces


def middle(query, keys, values, seg_all, cols, shards, gate_all, up_all, gains, tokens, out_grad,
           fsdp, ctx, n, seq_dev, late):
    rows, width = tokens.shape
    q_width = query.shape[1]
    heads = q_width // HEAD_DIM
    inner = gate_all.shape[0]
    tok_dev = rows // seq_dev
    per = tok_dev // TILE
    win, span = window(ctx, tok_dev), key_span(ctx, tok_dev)
    tiles = span + 1
    part = TILE if tiles <= 3 else 64
    chunk, hop = 32, 2
    size, piece = 256, 64
    per_block = size // piece
    half = rows // 2
    cols_at = width // 4
    block_shape = (inner, width // fsdp)
    count = 3

    def kernel(*refs):
        (q_in, k_in, v_in, segk, cols, wo_in, wd_in, wg_in, wu_in, gain, tok_in, cot_in), refs = refs[:12], refs[12:]
        (o_branch, o_feed, o_dmid, o_mid, o_wo, o_gain, o_bsq, o_mark, o_att, o_lse), refs = refs[:10], refs[10:]
        outs, refs = refs[:3], refs[3:]
        one, gsems, parts, refs = refs[:4], refs[4:6], refs[6:9], refs[9:]
        (query, keys, values, att, att_all, wo, wd, wg, wu, tok, cot), refs = refs[:11], refs[11:]
        (mid, r2, xn, hid, dg, du, p_two, p_feed, bsem), refs = refs[:9], refs[9:]
        bring = Bring([(q_in, query), (k_in, keys), (v_in, values), (tok_in, tok), (wg_in, wg), (wu_in, wu),
                       (cot_in, cot), (att, o_att), (p_feed, o_feed)], bsem)
        bring.start(range(7))
        meet(n, fsdp, ctx)
        line = LineGather(n, piece, att, att_all, *refs[:3])
        spread = Spread(fsdp, [(wo_in, wo), (wd_in, wd)], [1, 1], *refs[3:6])
        keep = refs[6:]
        spread.start()
        o_gain[...] = jnp.zeros_like(o_gain)
        o_bsq[...] = jnp.zeros_like(o_bsq)
        o_mark[...] = jnp.zeros_like(o_mark)
        g2 = gain.at[1:2]

        def back(at, own, total):
            middle_rows = mid[at, :]
            o_mid[own, :] = middle_rows
            unit = middle_rows * r2[at, :]
            o_gain[...] += jnp.sum((total * unit).reshape(chunk // 8, 8, width), axis=0)
            scaled = total * g2[...]
            mean = jnp.mean(scaled * unit, axis=-1, keepdims=True)
            d_mid = cot[at, :].astype(F32) + r2[at, :] * (scaled - unit * mean)
            o_dmid[own, :] = d_mid
            first_unit = tok[at, :].astype(F32) * cols[at, R_ONE : R_ONE + 1]
            o_mark[at, 0:1] = jnp.sum(first_unit * d_mid, axis=-1, keepdims=True)
            return d_mid.astype(BF16)

        first = LineSum(n, chunk, hop, p_two, one[0], one[1], o_branch, one[2], one[3], back)
        if late:
            held = [[out, None, None] for out in outs]
        else:
            held = [keep[3 * a : 3 * a + 3] for a in range(count)]
        grad = GradSum(fsdp, ctx, parts, [1] * count, outs, held, *gsems)
        bring.wait([0, 1, 2])

        def query_rows(i, j):
            seq = i // per
            q_tile = (win - 1) * per + lax.rem(i, per)
            at = pl.ds(pl.multiple_of(i * TILE + j * part, part), part)
            near = pl.ds(pl.multiple_of((seq * win * per + q_tile - span) * TILE, TILE), tiles * TILE)
            counted = jnp.concatenate(
                [
                    c.astype(F32)
                    for c in counted_keys(
                        cols, segk, at, seq, q_tile * TILE + j * part, q_tile - span, tiles, tok_dev, win
                    )
                ],
                axis=1,
            )
            accum = jnp.zeros((part, q_width), F32)
            lane = lax.broadcasted_iota(jnp.int32, (part, 128), 1)
            kept = jnp.zeros((part, 128), F32)
            for h in range(heads):
                score = jnp.where(counted > 0.0, dot_t(head_only(query[at, :], h), keys[near, :]) * 0.125, -1e30)
                top = jnp.max(score, axis=-1, keepdims=True)
                weight = jnp.exp(score - top)
                total = jnp.sum(weight, axis=-1, keepdims=True)
                prob = (weight * (1.0 / total)).astype(BF16)
                accum = accum + jnp.dot(prob, head_only(values[near, :], h), preferred_element_type=F32)
                kept = jnp.where(lane == h, top + jnp.log(total), kept)
                if part == TILE:
                    line.step((i - 1) * per_block + h * per_block // heads)
            o_lse[at, :] = kept
            att[at, :] = accum.astype(BF16)

        def query_tile(i):
            if part == TILE:
                query_rows(i, 0)
                return
            loop(0, TILE // part, lambda j: query_rows(i, j))
            for h in range(per_block):
                line.step((i - 1) * per_block + h)

        loop(0, rows // TILE, query_tile)
        bring.start([7])
        line.begin()
        s1 = (rows // TILE - 1) * per_block
        spread.relay()
        spread.finish()
        tp = lax.axis_index("tp")
        o_wo[...] = wo[pl.ds(pl.multiple_of(tp * q_width, q_width), q_width), :]
        line.begun()
        bring.wait([3, 4, 5, 6])

        def block_of_rows(b):
            at = pl.ds(pl.multiple_of(b * size, size), size)
            seq = b * size // tok_dev

            def steps(j):
                line.step(s1 + b * per_block + j)
                first.step((b - 1) * per_block + j)

            branch = dot(att_all[at, :], wo[...])
            middle_rows = tok[at, :].astype(F32) + branch
            mid[at, :] = middle_rows
            o_bsq[pl.ds(pl.multiple_of(seq * 8, 8), 8), :] += jnp.sum(
                (branch * branch * cols[at, VALID : VALID + 1]).reshape(size // 8, 8, width), axis=0
            )
            scale = lax.rsqrt(jnp.mean(middle_rows * middle_rows, axis=-1, keepdims=True) + eps)
            r2[at, :] = scale
            unit = (middle_rows * scale * g2[...]).astype(BF16)
            xn[at, :] = unit
            steps(0)
            gate = dot_t(unit, wg[...])
            upper = dot_t(unit, wu[...])
            sigma = jax.nn.sigmoid(gate)
            swish = gate * sigma
            hidden = (swish * upper).astype(BF16)
            hid[at, :] = hidden
            slope = upper * sigma * (1.0 + gate * (1.0 - sigma))
            steps(1)
            p_feed[at, :] = dot(hidden, wd[...]).astype(BF16)
            d_hidden = dot_t(cot[at, :], wd[...])
            d_gate = (d_hidden * slope).astype(BF16)
            d_upper = (d_hidden * swish).astype(BF16)
            dg[at, :] = d_gate
            du[at, :] = d_upper
            steps(2)
            p_two[at, :] = (dot(d_gate, wg[...]) + dot(d_upper, wu[...])).astype(BF16)
            steps(3)

        loop(0, rows // size, block_of_rows)
        bring.start([8])
        s0 = (rows // size - 1) * per_block

        def product(i):
            at = pl.ds(pl.multiple_of(i * cols_at, cols_at), cols_at)
            left = xn[:, at]
            parts[0][:, at] = dot_rows(dg[...], left).astype(BF16)
            parts[1][:, at] = dot_rows(du[...], left).astype(BF16)
            parts[2][:, at] = dot_rows(hid[...], cot[:, at]).astype(BF16)

        def busy(s):
            first.step(s)
            product(s - s0)

        loop(s0, s0 + 4, busy)
        grad.start()
        last = first.steps()
        loop(s0 + 4, s0 + 6, first.step)
        grad.pair()
        if not late:
            grad.second()
        loop(s0 + 6, last, first.step)
        if not late:
            grad.third()

            def store(a, at, total):
                outs[a][at, :] = total

            grad.fourth(store)
            grad.drain()
        line.drain()
        first.drain()
        grad.drain_pair()
        bring.wait([7, 8])

    ys = fsdp // 2
    out = pl.pallas_call(
        kernel,
        out_shape=(
            shape_of((rows, width), BF16),
            shape_of((rows, width), BF16),
            shape_of((half, width), F32),
            shape_of((half, width), F32),
            shape_of((q_width, width), BF16),
            shape_of((8, width), F32),
            shape_of((8 * seq_dev, width), F32),
            shape_of((rows, 128), F32),
            shape_of((rows, q_width), BF16),
            shape_of((rows, 128), F32),
        )
        + ((shape_of((ys,) + block_shape, BF16) if late else shape_of(block_shape, F32)),) * count,
        in_specs=[ANY] * 3 + [VMEM] * 4 + [ANY] * 2 + [VMEM] + [ANY] * 2,
        out_specs=(VMEM, ANY) + (VMEM,) * 6 + (ANY, VMEM) + (VMEM,) * count,
        scratch_shapes=LineSum.scratch(n, rows, width, chunk)
        + GradSum.semaphores(fsdp, ctx, count)
        + [pltpu.VMEM((inner, width), BF16)] * count
        + [
            pltpu.VMEM((rows, q_width), BF16),
            pltpu.VMEM((win * rows, q_width), BF16),
            pltpu.VMEM((win * rows, q_width), BF16),
            pltpu.VMEM((rows, q_width), BF16),
            pltpu.VMEM((rows, n * q_width), BF16),
            pltpu.VMEM((n * q_width, width), BF16),
            pltpu.VMEM((inner, width), BF16),
            pltpu.VMEM((inner, width), BF16),
            pltpu.VMEM((inner, width), BF16),
            pltpu.VMEM((rows, width), BF16),
            pltpu.VMEM((rows, width), BF16),
            pltpu.VMEM((rows, width), F32),
            pltpu.VMEM((rows, 1), F32),
            pltpu.VMEM((rows, width), BF16),
            pltpu.VMEM((rows, inner), BF16),
            pltpu.VMEM((rows, inner), BF16),
            pltpu.VMEM((rows, inner), BF16),
            pltpu.VMEM((rows, width), BF16),
            pltpu.VMEM((rows, width), BF16),
            pltpu.SemaphoreType.DMA((9,)),
        ]
        + LineGather.scratch(n, rows // piece)
        + Spread.scratch(fsdp, 2)
        + ([] if late else GradSum.scratch(fsdp, ctx, [block_shape] * count)),
        compiler_params=params(2, 64),
    )(query, keys, values, seg_all, cols, *shards, gate_all, up_all, gains, tokens, out_grad)
    return out[:10], out[10:]


def back(query, keys, values, seg_all, cols, lse, attended, d_branch, wo_rows, weights, lat_all, xn_one, gains,
         tokens, d_middle, mid_own, part_feed, marks, gain_part, branch_sq, firsts, fsdp, ctx, n, seq_dev):
    rows, width = tokens.shape
    w_qry, w_lat, w_kproj, w_vproj = weights
    q_width, latent = query.shape[1], w_lat.shape[1]
    heads, tok_dev = q_width // HEAD_DIM, rows // seq_dev
    per = tok_dev // TILE
    win, span = window(ctx, tok_dev), key_span(ctx, tok_dev)
    tiles = span + 1
    group = tiles if tiles <= 3 else 1
    chunk, hop, wide, side = 32, 2, 256, 128
    half = rows // 2
    axes = (0, 0, 0, 1, 0)
    whole = ((width, q_width), (latent, q_width), (latent, q_width), (q_width, width), (width, latent))
    blocks = [GradSum.block_shape(w, a, fsdp) for w, a in zip(whole, axes)]
    lat = blocks[-1]
    ffn = [f.shape[1:] for f in firsts]
    seq_pieces = tok_dev // wide
    many = max(width, rows)

    def kernel(*refs):
        (q_ref, k_ref, v_ref, segk, cols, lse_ref, att, dbr, wo), refs = refs[:9], refs[9:]
        (wq, wl, wk, wv, la_in, xn_in, gain, tok_in, dmid_in, mid_in, feed_in), refs = refs[:11], refs[11:]
        (marks, gain_two, bsq), fsts, refs = refs[:3], refs[3 : 3 + len(ffn)], refs[3 + len(ffn) :]
        (o_tok, o_mixed, o_small), outs, refs = refs[:3], refs[3:8], refs[8:]
        fouts, refs = refs[: len(ffn)], refs[len(ffn) :]
        one, two, keep, gsems, parts, refs = refs[:4], refs[4:8], refs[8:23], refs[23:25], refs[25:30], refs[30:]
        (p_one, dlat, came, c_recv, c_sent, gacc, sm, sacc), refs = refs[:8], refs[8:]
        (dk, dv, dq, dqb, grad_seq, lat_parts), refs = refs[:6], refs[6:]
        (la, xn, tok, dmid, mid, p_feed, bsem), refs = refs[:7], refs[7:]
        (lat_own, lat_every), lsems, sums, refs = refs[:2], refs[2:5], refs[5:14], refs[14:]
        bring = Bring([(feed_in, p_feed), (mid_in, mid), (la_in, la), (xn_in, xn), (tok_in, tok), (dmid_in, dmid)], bsem)
        bring.start()
        meet(n, fsdp, ctx, everyone=True)
        x = lax.axis_index("ctx")
        own_shard = win - 1
        grad_ffn = None
        if ffn:
            fkeep, fsems = refs[: 2 * len(ffn)], refs[2 * len(ffn) :]
            grad_ffn = GradSum(fsdp, ctx, [], [], fouts,
                               [[fsts[a], fkeep[2 * a], fkeep[2 * a + 1]] for a in range(len(ffn))], *fsems)
            grad_ffn.second()
        gacc[...] = jnp.zeros_like(gacc)
        sacc[...] = jnp.zeros_like(sacc)
        sm[...] = jnp.zeros_like(sm)
        g1 = gain.at[0:1]

        def forward(at, own, total):
            mixed = mid[own, :] + total
            seq = at.start // tok_dev
            counted = cols[at, VALID : VALID + 1]
            sacc[seq] += jnp.sum((mixed * mixed * counted).reshape(chunk // 8, 8, width), axis=0)
            sacc[seq_dev + seq] += jnp.sum((total * total * counted).reshape(chunk // 8, 8, width), axis=0)
            return mixed.astype(BF16)

        def backward(at, own, total):
            r1 = cols[at, R_ONE : R_ONE + 1]
            unit = tok[at, :].astype(F32) * r1
            scaled = total * g1[...]
            mean = jnp.mean(scaled * unit, axis=-1, keepdims=True)
            return (dmid[own, :] + r1 * (scaled - unit * mean)).astype(BF16)

        feed = LineSum(n, chunk, hop, p_feed, two[0], two[1], o_mixed, two[2], two[3], forward)
        first = LineSum(n, chunk, hop, p_one, one[0], one[1], o_tok, one[2], one[3], backward)
        grad = GradSum(fsdp, ctx, parts, axes, outs, [keep[3 * a : 3 * a + 3] for a in range(5)], *gsems)
        line = RowGather(n, lat_own, lat_every, *lsems)
        over_tp = AxisSum("tp", n, *sums[0:3])
        over_ctx = AxisSum("ctx", ctx, *sums[3:6])
        over_fsdp = AxisSum("fsdp", fsdp, *sums[6:9])

        def clear(i):
            at = pl.ds(pl.multiple_of(i * TILE, TILE), TILE)
            dk[at, :] = jnp.zeros((TILE, q_width), F32)
            dv[at, :] = jnp.zeros((TILE, q_width), F32)

        loop(0, win * rows // TILE, clear)
        bring.wait([0, 1])

        def query_tile(i, step):
            seq = i // per
            q_tile = own_shard * per + lax.rem(i, per)
            at = pl.ds(pl.multiple_of(i * TILE, TILE), TILE)
            grad_seq[...] = dot_t(dbr[at, :], wo[...]).astype(BF16)
            product = grad_seq[...].astype(F32) * att[at, :].astype(F32)
            delta = [jnp.sum(head_only(product, h), axis=-1, keepdims=True) for h in range(heads)]
            dq[...] = jnp.zeros_like(dq)

            def key_tiles(kk):
                t = q_tile - span + kk * group
                near = pl.ds(pl.multiple_of((seq * win * per + t) * TILE, TILE), group * TILE)
                counted = jnp.concatenate(
                    [c.astype(F32) for c in counted_keys(cols, segk, at, seq, q_tile * TILE, t, group, tok_dev, win)], axis=1
                )
                kept = lse_ref[at, :]
                d_query = jnp.zeros((TILE, q_width), F32)
                d_key = jnp.zeros((group * TILE, q_width), F32)
                d_value = jnp.zeros((group * TILE, q_width), F32)
                for h in range(heads):
                    mine, ours = head_only(q_ref[at, :], h), head_only(grad_seq[...], h)
                    score = jnp.where(counted > 0.0, dot_t(mine, k_ref[near, :]) * 0.125, -1e30)
                    prob = jnp.exp(score - kept[:, h : h + 1]) * counted
                    d_score = (prob * (dot_t(ours, v_ref[near, :]) - delta[h])).astype(BF16)
                    d_query = d_query + jnp.dot(d_score, head_only(k_ref[near, :], h), preferred_element_type=F32)
                    d_key = d_key + dot_rows(d_score, mine)
                    d_value = d_value + dot_rows(prob.astype(BF16), ours)
                    step(kk * heads + h)
                dq[...] += d_query
                dk[near, :] += d_key * 0.125
                dv[near, :] += d_value

            loop(0, tiles // group, key_tiles)
            dqb[at, :] = (dq[...] * 0.125).astype(BF16)

        def latent_rows(shard, seq, i):
            return pl.ds(pl.multiple_of((seq * win + shard) * tok_dev + i * wide, wide), wide)

        def send(k, seq, i):
            at = pl.ds(pl.multiple_of(seq * tok_dev + i * wide, wide), wide)
            return remote(lat_parts.at[latent_rows(own_shard - k, seq, i)], came.at[k - 1, at],
                          c_sent.at[k - 1, seq, i], c_recv.at[k - 1, seq, i], {"ctx": x - k})

        def latents(seq):
            for k in range(win - 1, -1, -1):
                for i in range(seq_pieces):
                    at = latent_rows(own_shard - k, seq, i)
                    lat_parts[at, :] = (
                        dot_t(dk[at, :].astype(BF16), wk[...]) + dot_t(dv[at, :].astype(BF16), wv[...])
                    ).astype(BF16)
                    if k > 0:

                        @pl.when(x - k >= 0)
                        def _(k=k, i=i):
                            send(k, seq, i).start()

        def whole_latent(j):
            seq, i = j // seq_pieces, lax.rem(j, seq_pieces)
            at = pl.ds(pl.multiple_of(j * wide, wide), wide)
            dlat[at, :] = lat_parts[latent_rows(own_shard, seq, i), :]
            for k in range(1, win):

                @pl.when(x + k < ctx)
                def _(k=k):
                    wait_came(came.at[k - 1, at], c_sent.at[k - 1, seq, i], c_recv.at[k - 1, seq, i])
                    dlat[at, :] = (dlat[at, :].astype(F32) + came[k - 1, at, :].astype(F32)).astype(BF16)

            p_one[at, :] = (dot_t(dqb[at, :], wq[...]) + dot_t(dlat[at, :], wl[...])).astype(BF16)

        tile_steps = (tiles // group) * heads
        every = max(tile_steps // 4, 1)

        def sequence(seq):
            def tile(i):
                def step(j):
                    @pl.when(lax.rem(j, every) == 0)
                    def _():
                        feed.step(i * (tile_steps // every) + j // every)

                query_tile(i, step)

            loop(seq * per, seq * per + per, tile)
            latents(seq)

        loop(0, seq_dev, sequence)
        fed = seq_dev * per * (tile_steps // every)

        bring.wait([2, 3, 4, 5])

        def product(i):
            at = pl.ds(pl.multiple_of(i * wide, wide), wide)
            parts[0][at, :] = dot_rows(xn[:, at], dqb[...]).astype(BF16)
            parts[3][:, at] = dot_rows(att[...], dbr[:, at]).astype(BF16)

        def steps(s):
            first.step(s)
            feed.step(fed + s)

        early = (seq_dev - 1) * seq_pieces
        loop(0, early, whole_latent)

        def mixed_work(i):
            product(i)
            steps(i)

        loop(0, width // wide, mixed_work)
        s0 = width // wide
        if grad_ffn is not None:
            grad_ffn.third()
        parts[1][...] = dot_rows(la[...], dk[...].astype(BF16)).astype(BF16)
        parts[2][...] = dot_rows(la[...], dv[...].astype(BF16)).astype(BF16)
        loop(early, rows // wide, whole_latent)

        def product_lat(s):
            at = pl.ds(pl.multiple_of((s - s0) * wide, wide), wide)
            parts[4][at, :] = dot_rows(xn[:, at], dlat[...]).astype(BF16)
            steps(s)

        begun = s0 + width // wide
        loop(s0, begun, product_lat)
        grad.start()

        def gains_of(s):
            steps(s)
            at = pl.ds(pl.multiple_of((s - begun) * side, side), side)
            value = p_one[at, :].astype(F32) * (tok[at, :].astype(F32) * cols[at, R_ONE : R_ONE + 1])
            gacc[...] += jnp.sum(value.reshape(side // 8, 8, width), axis=0)
            along = lax.dot_general(jnp.ones((8, width), F32), value * g1[...], (((1,), (1,)), ((), ())),
                                    precision=lax.Precision.HIGHEST, preferred_element_type=F32)
            sm[3:4, at] = along[0:1, :]
            sm[4:5, at] = marks[at, :].T[0:1, :]
            sm[5:6, at] = cols[at, :].T[R_ONE : R_ONE + 1, :]

        mark = begun + rows // side
        loop(begun, begun + 1, gains_of)
        grad.pair()
        grad.second()
        loop(begun + 1, begun + 4, gains_of)
        grad.third()
        loop(begun + 4, mark, gains_of)
        last = first.steps()
        for s in range(fed + mark, feed.steps()):
            feed.step(s)
        lane = lax.broadcasted_iota(jnp.int32, (1, many), 1)
        once = jnp.where(lax.axis_index("tp") == 0, 1.0, 0.0)
        row = jnp.zeros((1, many), F32)

        def whole_sum(value):
            return jnp.sum(jnp.sum(value, axis=0, keepdims=True), axis=1, keepdims=True)

        for q in range(seq_dev):
            values = [
                whole_sum(sacc[q]),
                whole_sum(sacc[seq_dev + q]),
                whole_sum(bsq[8 * q : 8 * q + 8, :]) * once,
                jnp.sum(cols[q * tok_dev : (q + 1) * tok_dev, VALID : VALID + 1], axis=0, keepdims=True) * once,
            ]
            for j, value in enumerate(values):
                row = row + jnp.where(lane == 4 * q + j, value, 0.0)
        sm[2:3, :] = row
        sm[0:1, 0:width] = jnp.sum(gacc[...], axis=0, keepdims=True)
        sm[1:2, 0:width] = jnp.sum(gain_two[...], axis=0, keepdims=True)
        r_row = sm[5:6, :]
        over_tp.start(sm[...])

        def store(a, at, total):
            if a < 4:
                outs[a][at, :] = total
            else:
                lat_own[at, :] = total.astype(BF16)

        def store_ffn(a, at, total):
            fouts[a][at, :] = total

        grad.fourth(store)
        line.start()
        loop(mark, mark + 2, steps)
        line.relay([1])
        along_tp = over_tp.finish()
        over_ctx.start(along_tp)
        loop(mark + 2, mark + 4, steps)
        if n > 2:
            line.relay([2])
        along_ctx = over_ctx.finish()
        over_fsdp.start(along_ctx)
        if grad_ffn is not None:
            grad_ffn.fourth(store_ffn)
        loop(mark + 4, last, steps)
        if n > 3:
            line.relay(range(3, n))
        everywhere = over_fsdp.finish()
        row = lax.broadcasted_iota(jnp.int32, everywhere.shape, 0)
        o_small[...] = jnp.where(row < 2, everywhere, along_ctx)
        o_small[3:4, :] = (along_tp[4:5] + eps * r_row * r_row * r_row * along_tp[3:4]) * (1.0 / width**0.5)
        line.finish()

        def gather(i):
            at = pl.ds(pl.multiple_of(i * 16, 16), 16)
            for g in range(GROUPS):
                total = jnp.zeros((16, lat[1]), F32)
                for t in range(n):
                    if t * GROUPS // n == g:
                        total = total + lat_every[t, at, :].astype(F32)
                outs[4][at, g * lat[1] : (g + 1) * lat[1]] = total

        loop(0, lat[0] // 16, gather)
        for k in range(1, win):

            @pl.when(x - k >= 0)
            def _(k=k):
                for seq in range(seq_dev):
                    for i in range(seq_pieces):
                        send(k, seq, i).wait_send()

        feed.drain()
        first.drain()
        grad.drain_pair()
        grad.drain()
        if grad_ffn is not None:
            grad_ffn.drain()

    out = pl.pallas_call(
        kernel,
        out_shape=(
            shape_of((rows, width), BF16),
            shape_of((rows, width), BF16),
            shape_of((8, many), F32),
        )
        + tuple(shape_of(b, F32) for b in blocks[:-1])
        + (shape_of((lat[0], GROUPS * lat[1]), F32),)
        + tuple(shape_of(f, F32) for f in ffn),
        in_specs=[VMEM] * 13 + [ANY] * 2 + [VMEM] + [ANY] * 4 + [VMEM] * (3 + len(ffn)),
        out_specs=(VMEM,) * (8 + len(ffn)),
        scratch_shapes=LineSum.scratch(n, rows, width, chunk) * 2
        + GradSum.scratch(fsdp, ctx, blocks)
        + GradSum.semaphores(fsdp, ctx, 5)
        + [pltpu.VMEM(w, BF16) for w in whole]
        + [
            pltpu.VMEM((rows, width), BF16),
            pltpu.VMEM((rows, latent), BF16),
            pltpu.VMEM((max(win - 1, 1), rows, latent), BF16),
            pltpu.SemaphoreType.DMA((max(win - 1, 1), seq_dev, seq_pieces)),
            pltpu.SemaphoreType.DMA((max(win - 1, 1), seq_dev, seq_pieces)),
            pltpu.VMEM((8, width), F32),
            pltpu.VMEM((8, many), F32),
            pltpu.VMEM((2 * seq_dev, 8, width), F32),
            pltpu.VMEM((win * rows, q_width), F32),
            pltpu.VMEM((win * rows, q_width), F32),
            pltpu.VMEM((TILE, q_width), F32),
            pltpu.VMEM((rows, q_width), BF16),
            pltpu.VMEM((TILE, q_width), BF16),
            pltpu.VMEM((win * rows, latent), BF16),
        ]
        + [
            pltpu.VMEM((win * rows, latent), BF16),
            pltpu.VMEM((rows, width), BF16),
            pltpu.VMEM((rows, width), BF16),
            pltpu.VMEM((half, width), F32),
            pltpu.VMEM((half, width), F32),
            pltpu.VMEM((rows, width), BF16),
            pltpu.SemaphoreType.DMA((6,)),
        ]
        + [pltpu.VMEM(lat, BF16), pltpu.VMEM((n,) + lat, BF16)]
        + RowGather.scratch(n)
        + AxisSum.scratch(n, (8, many))
        + AxisSum.scratch(ctx, (8, many))
        + AxisSum.scratch(fsdp, (8, many))
        + (GradSum.scratch(fsdp, ctx, ffn, False) + GradSum.semaphores(fsdp, ctx, len(ffn)) if ffn else []),
        compiler_params=params(3, 64),
    )(query, keys, values, seg_all, cols, lse, attended, d_branch, wo_rows, w_qry, w_lat, w_kproj, w_vproj,
      lat_all, xn_one, gains, tokens, d_middle, mid_own, part_feed, marks, gain_part, branch_sq, *firsts)
    return out[:3], out[3:8], out[8:]


def publish(arrays, small, seq_dev, tok_dev, feat_dim, fsdp):
    count = len(arrays)
    per = feat_dim // fsdp

    def kernel(*refs):
        srcs, sm, refs = refs[:count], refs[count], refs[count + 1 :]
        dsts, (gains, stats, radial), refs = refs[:count], refs[count : count + 3], refs[count + 3 :]
        inward = Bring(list(zip(srcs, refs[:count])), refs[count])
        outward = Bring(list(zip(refs[:count], dsts)), refs[count + 1])
        inward.start()
        f = lax.axis_index("fsdp")
        gains[...] = sm[0:2, pl.ds(pl.multiple_of(f * per, per), per)]
        for q in range(seq_dev):
            radial[q : q + 1, :] = sm[3:4, q * tok_dev : (q + 1) * tok_dev]
            total = sm[2:3, 4 * q + 3 : 4 * q + 4] * feat_dim
            for j, lane in enumerate((0, 2, 1)):
                stats[q : q + 1, j : j + 1] = jnp.sqrt(sm[2:3, 4 * q + lane : 4 * q + lane + 1] / total)
        for i in range(count):
            inward.wait([i])
            outward.start([i])
        outward.wait()

    out = pl.pallas_call(
        kernel,
        out_shape=tuple(shape_of(a.shape, a.dtype) for a in arrays)
        + (shape_of((2, per), F32), shape_of((seq_dev, 3), F32), shape_of((seq_dev, tok_dev), F32)),
        in_specs=[ANY] * count + [VMEM],
        out_specs=(ANY,) * count + (VMEM,) * 3,
        scratch_shapes=[pltpu.VMEM(a.shape, a.dtype) for a in arrays] + [pltpu.SemaphoreType.DMA((count,))] * 2,
        compiler_params=pltpu.CompilerParams(vmem_limit_bytes=60 << 20),
    )(*arrays, small)
    return out[:count], out[count], out[count + 1], out[count + 2]


def on_device(
    tokens, gain1, w_latent, w_query, w_key, w_value, w_out, gain2, w_gate, w_up, w_down, segments, cotangent
):
    seq_dev, tok_dev, feat_dim = tokens.shape
    n_ctx, n_tp, n_fsdp = lax.axis_size("ctx"), lax.axis_size("tp"), lax.axis_size("fsdp")
    row_count = seq_dev * tok_dev
    tok_rows = tokens.reshape(row_count, feat_dim)
    out_grad = cotangent.reshape(row_count, feat_dim)
    (xn_one, cols, gains, w_lat, w_qry, w_kproj, w_vproj, gate_all, up_all, wo_cols, seg_all, lat_all,
     query, keys, values) = front(
        tok_rows, gain1, gain2, w_latent, (w_query, w_key, w_value), w_out, (w_gate.T, w_up.T), segments,
        n_fsdp, n_ctx, n_tp,
    )
    late = window(n_ctx, tok_dev) <= 2
    (d_branch, part_feed, d_middle, mid_own, wo_rows, gain_part, branch_sq, marks, attended, lse), ffn = middle(
        query, keys, values, seg_all, cols, (wo_cols.reshape(-1, w_out.shape[1]), w_down), gate_all, up_all, gains,
        tok_rows, out_grad, n_fsdp, n_ctx, n_tp, seq_dev, late,
    )
    (grad_tokens, mixed, small), (s_qry, s_kproj, s_vproj, s_outp, s_lat), late_ffn = back(
        query, keys, values, seg_all, cols, lse, attended, d_branch, wo_rows, (w_qry, w_lat, w_kproj, w_vproj),
        lat_all, xn_one, gains, tok_rows, d_middle, mid_own, part_feed, marks, gain_part, branch_sq,
        ffn if late else (), n_fsdp, n_ctx, n_tp, seq_dev,
    )
    s_gate, s_up, s_down = late_ffn if late else ffn
    arrays, gain_grads, stats, radial = publish(
        (mixed, grad_tokens, s_lat, s_qry, s_kproj, s_vproj, s_outp, s_gate, s_up, s_down), small,
        seq_dev, tok_dev, feat_dim, n_fsdp,
    )
    mixed, grad_tokens, s_lat, s_qry, s_kproj, s_vproj, s_outp, s_gate, s_up, s_down = arrays
    return (
        mixed.reshape(seq_dev, tok_dev, feat_dim),
        grad_tokens.reshape(seq_dev, tok_dev, feat_dim),
        gain_grads[0],
        s_lat,
        s_qry,
        s_kproj,
        s_vproj,
        s_outp,
        gain_grads[1],
        s_gate.T,
        s_up.T,
        s_down,
        stats,
        radial,
    )


def solution(mesh):
    return jax.shard_map(
        on_device,
        mesh=mesh,
        in_specs=(
            P("fsdp", "ctx", None),
            P("fsdp"),
            P("fsdp", None),
            P("fsdp", "tp"),
            P("fsdp", "tp"),
            P("fsdp", "tp"),
            P("tp", "fsdp"),
            P("fsdp"),
            P("fsdp", "tp"),
            P("fsdp", "tp"),
            P("tp", "fsdp"),
            P("fsdp", "ctx"),
            P("fsdp", "ctx", None),
        ),
        out_specs=(
            P("fsdp", "ctx", None),
            P("fsdp", "ctx", None),
            P("fsdp"),
            P("fsdp", None),
            P("fsdp", "tp"),
            P("fsdp", "tp"),
            P("fsdp", "tp"),
            P("tp", "fsdp"),
            P("fsdp"),
            P("fsdp", "tp"),
            P("fsdp", "tp"),
            P("tp", "fsdp"),
            P("fsdp", None),
            P("fsdp", "ctx"),
        ),
        check_vma=False,
    )
```

profile of v0, /device:TPU:0, one launch (start us, length us, event | category | flops | bytes accessed | tf_op | source)
XLA Modules:
  0.0 288.8 jit_solution(4529859640748821117)
XLA Ops:
  0.6 34.0 %shard_map.236 = (bf16[1024,1024]{1,0:T(8,128)(2,1)}, f32[1024,128]{1,0:T(8,128)}, f32[8,1024]{1,0:T(8,128)}, bf16[1024,256]{1,0:T(8,128)(2,1)}, bf16[1024,256]{...) custom-call(bf16[1024,1024]{1,0:T(8,128)(2,1)} %bitcast.11, ...), custom_call_target="tpu_custom_call" | custom-call | tf_op jit(solution)/shard_map/pallas_call | solution.py:776
  34.6 116.0 %shard_map.237 = (bf16[1024,1024]{1,0:T(8,128)(2,1)}, bf16[1024,1024]{1,0:T(8,128)(2,1)}, f32[512,1024]{1,0:T(8,128)}, f32[512,1024]{1,0:T(8,128)}, bf16[256,102...) custom-call(bf16[1024,256]{1,0:T(8,128)(2,1)} %get-tuple-element.66., ...), custom_call_target="tpu_custom_call" | custom-call | tf_op jit(solution)/shard_map/pallas_call | solution.py:1009
  150.6 129.7 %shard_map.238 = (bf16[1024,1024]{1,0:T(8,128)(2,1)}, bf16[1024,1024]{1,0:T(8,128)(2,1)}, f32[8,1024]{1,0:T(8,128)}, f32[256,256]{1,0:T(8,128)}, f32[64,256]{1,0...) custom-call(bf16[1024,256]{1,0:T(8,128)(2,1)} %get-tuple-element.66., ...), custom_call_target="tpu_custom_call" | custom-call | tf_op jit(solution)/shard_map/pallas_call | solution.py:1358
  280.4 7.1 %shard_map.239 = (bf16[1024,1024]{1,0:T(8,128)(2,1)}, bf16[1024,1024]{1,0:T(8,128)(2,1)}, f32[256,512]{1,0:T(8,128)}, f32[256,256]{1,0:T(8,128)}, f32[64,256]{1,...) custom-call(bf16[1024,1024]{1,0:T(8,128)(2,1)} %get-tuple-element.94, ...), custom_call_target="tpu_custom_call" | custom-call | tf_op jit(solution)/shard_map/pallas_call | solution.py:1433
  287.5 1.3 fusion
where the time goes:
time: 289 us
  Pallas kernels  287 us (99%)
    pallas_call x1, Pallas kernels, back(): pl.pallas_call(kernel, out_shape=(shape_of((rows, width), BF16), shape_of...  130 us
    pallas_call x1, Pallas kernels, middle(): pl.pallas_call(kernel, out_shape=(shape_of((rows, width), BF16), shape_of...  116 us
    pallas_call x1, Pallas kernels, front(): pl.pallas_call(kernel, out_shape=(shape_of((rows, width), BF16), shape_of...  34 us
    pallas_call x1, Pallas kernels, publish(): pl.pallas_call(kernel, out_shape=tuple((shape_of(a.shape, a.dtype) for a...  7.11 us

commit v1 on v0

--- a/solution.py
+++ b/solution.py
@@ -1,3 +1,5 @@
+from types import SimpleNamespace
+
 import jax
 import jax.numpy as jnp
 from jax import lax
@@ -186,15 +188,15 @@
 
 
 class LineGather:
-    def __init__(self, n, chunk, src, dst, recv, sent, own):
-        self.n, self.chunk, self.src, self.dst = n, chunk, src, dst
+    def __init__(self, n, chunk, src, dst, recv, sent, own, hop=1):
+        self.n, self.chunk, self.src, self.dst, self.hop = n, chunk, src, dst, hop
         self.width = src.shape[1]
         self.count = src.shape[0] // chunk
         self.recv, self.sent, self.own = recv, sent, own
         self.me = lax.axis_index("tp")
 
     def steps(self):
-        return self.count + self.n - 1
+        return self.count + self.hop * (self.n - 1)
 
     def columns(self, tp):
         return pl.ds(pl.multiple_of(tp * self.width, self.width), self.width)
@@ -226,7 +228,7 @@
                 remote(self.src.at[rows], self.place(me, s), self.sent.at[1], self.recv.at[me, s], right).start()
 
         for away in range(1, n):
-            at = s - away
+            at = s - away * self.hop
             for sign, onward in ((-1, right), (1, left)):
                 tp = me + sign * away
 
@@ -1442,6 +1444,734 @@
     return out[:count], out[count], out[count + 1], out[count + 2]
 
 
+class HalfSpread:
+    def __init__(self, fsdp, pairs, recv, sent, own):
+        self.fsdp, self.pairs, self.recv, self.sent, self.own = fsdp, pairs, recv, sent, own
+        self.f, self.x = lax.axis_index("fsdp"), lax.axis_index("ctx")
+        self.ys = fsdp // 2
+
+    def view(self, a, f, half=None):
+        src, dst = self.pairs[a]
+        rows, size = src.shape
+        columns = pl.ds(pl.multiple_of(f * size, size), size)
+        if half is None:
+            return dst.at[:, columns]
+        return dst.at[pl.ds(pl.multiple_of(half * (rows // 2), rows // 2), rows // 2), columns]
+
+    def part(self, a):
+        src = self.pairs[a][0]
+        return src.at[pl.ds(pl.multiple_of(self.x * (src.shape[0] // 2), src.shape[0] // 2), src.shape[0] // 2)]
+
+    def start(self, which):
+        for a in which:
+            for k in range(1, self.ys):
+                remote(self.part(a), self.view(a, self.f, self.x), self.sent.at[a, 0, k], self.recv.at[a, 0, k],
+                       {"fsdp": lax.rem(self.f + 2 * k, self.fsdp)}).start()
+        for a in which:
+            src = self.pairs[a][0]
+            remote(src, self.view(a, self.f), self.sent.at[a, 1, 0], self.recv.at[a, 1, 0],
+                   {"fsdp": sibling(self.f)}).start()
+            pltpu.make_async_copy(src, self.view(a, self.f), self.own.at[a]).start()
+
+    def source(self, k):
+        return lax.rem(self.f - 2 * k + self.fsdp, self.fsdp)
+
+    def relay(self, which):
+        for a in which:
+            for k in range(1, self.ys):
+                here = self.view(a, self.source(k), self.x)
+                wait_came(here, self.sent.at[a, 0, k], self.recv.at[a, 0, k])
+                remote(here, here, self.sent.at[a, 2, k], self.recv.at[a, 2, k], {"ctx": 1 - self.x}).start()
+                remote(here, here, self.sent.at[a, 3, k], self.recv.at[a, 3, k],
+                       {"fsdp": sibling(self.f)}).start()
+
+    def cross(self, which):
+        for a in which:
+            for k in range(1, self.ys):
+                here = self.view(a, self.source(k), 1 - self.x)
+                wait_came(here, self.sent.at[a, 2, k], self.recv.at[a, 2, k])
+                remote(here, here, self.sent.at[a, 4, k], self.recv.at[a, 4, k],
+                       {"fsdp": sibling(self.f)}).start()
+
+    def finish(self, which):
+        for a in which:
+            src = self.pairs[a][0]
+            other = sibling(self.f)
+            wait_came(self.view(a, other), self.sent.at[a, 1, 0], self.recv.at[a, 1, 0])
+            pltpu.make_async_copy(src, self.view(a, self.f), self.own.at[a]).wait()
+            for k in range(1, self.ys):
+                there = lax.rem(other - 2 * k + self.fsdp, self.fsdp)
+                wait_came(self.view(a, there, self.x), self.sent.at[a, 3, k], self.recv.at[a, 3, k])
+                wait_came(self.view(a, there, 1 - self.x), self.sent.at[a, 4, k], self.recv.at[a, 4, k])
+
+    def drain(self, which):
+        for a in which:
+            wait_sent(self.view(a, self.f), self.sent.at[a, 1, 0], self.recv.at[a, 1, 0])
+            for k in range(1, self.ys):
+                for kind in (0, 2, 3, 4):
+                    wait_sent(self.part(a), self.sent.at[a, kind, k], self.recv.at[a, kind, k])
+
+    @staticmethod
+    def scratch(fsdp, arrays):
+        return [
+            pltpu.SemaphoreType.DMA((arrays, 5, fsdp // 2)),
+            pltpu.SemaphoreType.DMA((arrays, 5, fsdp // 2)),
+            pltpu.SemaphoreType.DMA((arrays,)),
+        ]
+
+
+R_TWO, MARK, LSE = 3, 4, 8
+
+
+def layer(tokens, gain1, gain2, w_latent, shards, w_out, wide_shards, segments, out_grad, fsdp, ctx, n):
+    rows, width = tokens.shape
+    seq_dev, tok_dev = segments.shape
+    w_query = shards[0]
+    latent, q_width, inner = LATENT, w_query.shape[1], wide_shards[0].shape[0]
+    heads = q_width // HEAD_DIM
+    per = tok_dev // TILE
+    win, span = window(ctx, tok_dev), key_span(ctx, tok_dev)
+    own_shard = win - 1
+    tiles = span + 1
+    keyed = win * rows
+    per_group = HEADS // GROUPS * HEAD_DIM
+    wide, chunk = 128, 256
+    pieces = rows // chunk
+    per_seq = tok_dev // chunk
+    strip, hop, reach = 32, 2, 3
+    piece = 64
+    per_block = TILE // piece
+    side = 128
+    many = max(width, rows)
+    q_tiles = rows // TILE
+    steps_all = rows // 2 // strip
+    lag = hop * 2 * (n // 2)
+    ffn = (inner, width // fsdp)
+    axes = (0, 0, 0, 1, 0)
+    whole = ((width, q_width), (latent, q_width), (latent, q_width), (q_width, width), (width, latent))
+    blocks = [GradSum.block_shape(w, a, fsdp) for w, a in zip(whole, axes)]
+    lat = blocks[-1]
+    cols_at = width // 4
+
+    scratch = dict(
+        gbuf=pltpu.VMEM((8, gain1.shape[0]), F32),
+        sbuf=pltpu.VMEM((8, tok_dev), segments.dtype),
+        gain=pltpu.VMEM((8, width), F32),
+        segk=pltpu.VMEM((ctx, 8, tok_dev), segments.dtype),
+        cols=pltpu.VMEM((rows, 128), F32),
+        tok=pltpu.VMEM((rows, width), BF16),
+        gathered=pltpu.VMEM((rows, n * q_width), BF16),
+        wo=pltpu.VMEM((n * q_width, width), BF16),
+        cot=pltpu.VMEM((rows, width), BF16),
+        xn=pltpu.VMEM((rows, width), BF16),
+        p_two=pltpu.VMEM((rows, width), BF16),
+        p_feed=pltpu.VMEM((rows, width), BF16),
+        left=pltpu.VMEM((rows, width), BF16),
+        right=pltpu.VMEM((rows, width), BF16),
+        branch=pltpu.VMEM((rows, width), BF16),
+        mid=pltpu.VMEM((rows, width), F32),
+        wg=pltpu.VMEM((inner, width), BF16),
+        wu=pltpu.VMEM((inner, width), BF16),
+        wd=pltpu.VMEM((inner, width), BF16),
+        hid=pltpu.VMEM((rows, inner), BF16),
+        dg=pltpu.VMEM((rows, inner), BF16),
+        du=pltpu.VMEM((rows, inner), BF16),
+        w_lat=pltpu.VMEM((width, latent), BF16),
+        w_qry=pltpu.VMEM((width, q_width), BF16),
+        w_kproj=pltpu.VMEM((latent, q_width), BF16),
+        w_vproj=pltpu.VMEM((latent, q_width), BF16),
+        wo_rows=pltpu.VMEM((q_width, width), BF16),
+        wo_line=pltpu.VMEM((n,) + w_out.shape, BF16),
+        lat_all=pltpu.VMEM((keyed, latent), BF16),
+        query=pltpu.VMEM((rows, q_width), BF16),
+        keys=pltpu.VMEM((keyed, q_width), BF16),
+        values=pltpu.VMEM((keyed, q_width), BF16),
+        att=pltpu.VMEM((rows, q_width), BF16),
+        dk=pltpu.VMEM((keyed, q_width), F32),
+        dv=pltpu.VMEM((keyed, q_width), F32),
+        dqb=pltpu.VMEM((rows, q_width), BF16),
+        grad_seq=pltpu.VMEM((TILE, q_width), BF16),
+        lat_parts=pltpu.VMEM((keyed, latent), BF16),
+        dlat=pltpu.VMEM((rows, latent), BF16),
+        came=pltpu.VMEM((rows, latent), BF16),
+        g_sum=pltpu.VMEM((8, width), F32),
+        g_sum2=pltpu.VMEM((8, width), F32),
+        sm=pltpu.VMEM((8, many), F32),
+        sacc=pltpu.VMEM((3 * seq_dev, 8, width), F32),
+        lat_own=pltpu.VMEM(lat, BF16),
+        lat_every=pltpu.VMEM((n,) + lat, BF16),
+        local=pltpu.SemaphoreType.DMA((2,)),
+        flush=pltpu.SemaphoreType.DMA((10,)),
+        lat_recv=pltpu.SemaphoreType.DMA((pieces,)),
+        lat_sent=pltpu.SemaphoreType.DMA((pieces,)),
+        c_recv=pltpu.SemaphoreType.DMA((seq_dev, per_seq)),
+        c_sent=pltpu.SemaphoreType.DMA((seq_dev, per_seq)),
+    )
+    out_blocks = [shape_of(b, F32) for b in blocks[:-1]] + [shape_of((lat[0], GROUPS * lat[1]), F32)]
+    out_blocks += [shape_of(ffn, F32)] * 3
+    groups = dict(
+        outs=[pltpu.VMEM(o.shape, F32) for o in out_blocks[:5]],
+        held=GradSum.scratch(fsdp, ctx, [ffn] * 3 + blocks),
+        parts=[pltpu.VMEM(w, BF16) for w in whole],
+        spread=Spread.scratch(fsdp, 5),
+        half=HalfSpread.scratch(fsdp, 4),
+        share=CtxShare.scratch(ctx),
+        wline=RowGather.scratch(n),
+        gather=LineGather.scratch(n, rows // piece),
+        two=LineSum.scratch(n, rows, width, strip)[2:],
+        feed=LineSum.scratch(n, rows, width, strip)[2:],
+        one=LineSum.scratch(n, rows, width, strip)[2:],
+        gffn=GradSum.semaphores(fsdp, ctx, 3),
+        gatt=GradSum.semaphores(fsdp, ctx, 5),
+        lline=RowGather.scratch(n),
+        s_tp=AxisSum.scratch(n, (8, many)),
+        s_ctx=AxisSum.scratch(ctx, (8, many)),
+        s_fsdp=AxisSum.scratch(fsdp, (8, many)),
+    )
+    names = list(scratch)
+    shapes = list(scratch.values())
+    places = {}
+    for key, some in groups.items():
+        places[key] = (len(shapes), len(shapes) + len(some))
+        shapes = shapes + list(some)
+
+    def kernel(*refs):
+        (tok_in, ga, gb, wlat, wq, wkp, wvp, wout, wgt, wut, wdn, seg, cot_in), refs = refs[:13], refs[13:]
+        (o_mixed, o_tok), o_blocks, o_small, refs = refs[:2], refs[2:10], refs[10], refs[11:]
+        r = SimpleNamespace(**dict(zip(names, refs)))
+        g = SimpleNamespace(**{key: refs[a:b] for key, (a, b) in places.items()})
+        cols, tok, cot, xn, mid = r.cols, r.tok, r.cot, r.xn, r.mid
+        gain, segk = r.gain, r.segk
+        x, me = lax.axis_index("ctx"), lax.axis_index("tp")
+        outs = list(g.outs) + [mid.at[0 : ffn[0], i * ffn[1] : (i + 1) * ffn[1]] for i in range(3)]
+
+        load = Bring([(tok_in, tok), (cot_in, cot)], r.local)
+        load.start()
+        r.gbuf[...] = jnp.zeros_like(r.gbuf)
+        r.gbuf[0:1, :] = ga[...].astype(F32).reshape(1, -1)
+        r.gbuf[1:2, :] = gb[...].astype(F32).reshape(1, -1)
+        r.sbuf[...] = jnp.zeros_like(r.sbuf)
+        r.sbuf[0:seq_dev, :] = seg[...]
+        meet(n, fsdp, ctx, everyone=True)
+
+        group = me * q_width // per_group
+        src_lat = wlat.at[:, pl.ds(pl.multiple_of(group * latent, latent), latent)]
+        spread = Spread(
+            fsdp,
+            [(r.gbuf, gain), (src_lat, r.w_lat), (wq, r.w_qry), (wkp, r.w_kproj), (wvp, r.w_vproj)],
+            [1, 0, 0, 0, 0], *g.spread,
+        )
+        share = CtxShare(ctx, r.sbuf, segk, *g.share)
+        wline = RowGather(n, wout, r.wo_line, *g.wline)
+        half = HalfSpread(
+            fsdp,
+            [(wgt, r.wg), (wut, r.wu), (wdn, r.wd), (r.wo_line.reshape(n * q_width, w_out.shape[1]), r.wo)],
+            *g.half,
+        )
+        spread.start()
+        share.start()
+        wline.start()
+        half.start([0, 1, 2])
+        cols[...] = jnp.zeros_like(cols)
+        r.g_sum[...] = jnp.zeros_like(r.g_sum)
+        r.g_sum2[...] = jnp.zeros_like(r.g_sum2)
+        r.sacc[...] = jnp.zeros_like(r.sacc)
+        r.sm[...] = jnp.zeros_like(r.sm)
+        load.wait([0])
+
+        def scale(i):
+            at = pl.ds(pl.multiple_of(i * wide, wide), wide)
+            value = tok[at, :].astype(F32)
+            cols[at, R_ONE : R_ONE + 1] = lax.rsqrt(jnp.mean(value * value, axis=-1, keepdims=True) + eps)
+
+        loop(0, rows // wide, scale)
+        spread.relay([0, 1])
+        spread.finish([0, 1])
+        lat_all = r.lat_all
+
+        def place(shard, i):
+            seq = i // per_seq
+            return pl.ds(pl.multiple_of((seq * win + shard) * tok_dev + lax.rem(i, per_seq) * chunk, chunk), chunk)
+
+        def pass_on(i):
+            return remote(lat_all.at[place(own_shard, i)], lat_all.at[place(own_shard - 1, i)], r.lat_sent.at[i],
+                          r.lat_recv.at[i], {"ctx": x + 1})
+
+        def first_norm(i):
+            at = pl.ds(pl.multiple_of(i * chunk, chunk), chunk)
+            unit = (tok[at, :].astype(F32) * cols[at, R_ONE : R_ONE + 1] * gain[0:1, :]).astype(BF16)
+            xn[at, :] = unit
+            lat_all[place(own_shard, i), :] = dot(unit, r.w_lat[...]).astype(BF16)
+
+            @pl.when(x + 1 < ctx)
+            def _():
+                pass_on(i).start()
+
+        loop(0, pieces, first_norm)
+        wline.relay([1])
+        spread.relay([2, 3, 4])
+        spread.finish([2, 3, 4])
+
+        def project(shard, i):
+            to = place(shard, i)
+            value = lat_all[to, :]
+            r.keys[to, :] = dot(value, r.w_kproj[...]).astype(BF16)
+            r.values[to, :] = dot(value, r.w_vproj[...]).astype(BF16)
+
+        def ask(i):
+            at = pl.ds(pl.multiple_of(i * chunk, chunk), chunk)
+            r.query[at, :] = dot(xn[at, :], r.w_qry[...]).astype(BF16)
+            project(own_shard, i)
+
+        loop(0, pieces, ask)
+        if n > 2:
+            wline.relay([2])
+        share.finish()
+        for q in range(seq_dev):
+            at = slice(q * tok_dev, (q + 1) * tok_dev)
+            ids = jnp.broadcast_to(r.sbuf[q : q + 1, :].astype(F32), (128, tok_dev)).T
+            cols[at, SEGMENT : SEGMENT + 1] = ids[:, 0:1]
+            final = segk[ctx - 1, q : q + 1, tok_dev - 1 : tok_dev].astype(F32)
+            cols[at, VALID : VALID + 1] = jnp.where(ids[:, 0:1] != final, 1.0, 0.0)
+        if n > 3:
+            wline.relay(range(3, n))
+        wline.finish()
+        half.start([3])
+        half.relay([0, 1])
+
+        def theirs(i):
+            @pl.when(x - 1 >= 0)
+            def _():
+                wait_came(lat_all.at[place(own_shard - 1, i)], r.lat_sent.at[i], r.lat_recv.at[i])
+
+            @pl.when(x - 1 < 0)
+            def _():
+                lat_all[place(own_shard - 1, i), :] = jnp.zeros((chunk, latent), BF16)
+
+            project(own_shard - 1, i)
+
+        loop(0, pieces, theirs)
+
+        att, gathered = r.att, r.gathered
+        line = LineGather(n, piece, att, gathered, *g.gather, hop=reach)
+
+        def query_tile(i):
+            seq = i // per
+            q_tile = own_shard * per + lax.rem(i, per)
+            at = pl.ds(pl.multiple_of(i * TILE, TILE), TILE)
+            near = pl.ds(pl.multiple_of((seq * win * per + q_tile - span) * TILE, TILE), tiles * TILE)
+            counted = jnp.concatenate(
+                [
+                    c.astype(F32)
+                    for c in counted_keys(cols, segk, at, seq, q_tile * TILE, q_tile - span, tiles, tok_dev, win)
+                ],
+                axis=1,
+            )
+            accum = jnp.zeros((TILE, q_width), F32)
+            for h in range(heads):
+                score = dot_t(head_only(r.query[at, :], h), r.keys[near, :]) * 0.125
+                score = jnp.where(counted > 0.0, score, -1e30)
+                top = jnp.max(score, axis=-1, keepdims=True)
+                weight = jnp.exp(score - top)
+                total = jnp.sum(weight, axis=-1, keepdims=True)
+                prob = (weight * (1.0 / total)).astype(BF16)
+                accum = accum + jnp.dot(prob, head_only(r.values[near, :], h), preferred_element_type=F32)
+                cols[at, LSE + h : LSE + h + 1] = top + jnp.log(total)
+                line.step((i - 1) * per_block + h * per_block // heads)
+            att[at, :] = accum.astype(BF16)
+
+        loop(0, q_tiles, query_tile)
+        s1 = (q_tiles - 1) * per_block
+        line.begin()
+        half.relay([2, 3])
+        half.cross([0, 1, 2, 3])
+        loop(s1, per_block + reach * (n - 1), line.step)
+        s1 = per_block + reach * (n - 1)
+        half.finish([3, 0, 1, 2])
+        half.drain([0, 1, 2, 3])
+        r.wo_rows[...] = r.wo[pl.ds(pl.multiple_of(me * q_width, q_width), q_width), :]
+        line.begun()
+        load.wait([1])
+
+        p_two, p_feed, wg, wu, wd = r.p_two, r.p_feed, r.wg, r.wu, r.wd
+
+        def second_back(at, own, total):
+            unit = mid[at, :] * cols[at, R_TWO : R_TWO + 1]
+            r.g_sum2[...] += jnp.sum((total * unit).reshape(strip // 8, 8, width), axis=0)
+            scaled = total * gain[1:2, :]
+            mean = jnp.mean(scaled * unit, axis=-1, keepdims=True)
+            d_mid = cot[at, :].astype(F32) + cols[at, R_TWO : R_TWO + 1] * (scaled - unit * mean)
+            first_unit = tok[at, :].astype(F32) * cols[at, R_ONE : R_ONE + 1]
+            cols[at, MARK : MARK + 1] = jnp.sum(first_unit * d_mid, axis=-1, keepdims=True)
+            return d_mid.astype(BF16)
+
+        def forward(at, own, total):
+            mixed = mid[at, :] + total
+            seq = at.start // tok_dev
+            counted = cols[at, VALID : VALID + 1]
+            r.sacc[seq] += jnp.sum((mixed * mixed * counted).reshape(strip // 8, 8, width), axis=0)
+            r.sacc[seq_dev + seq] += jnp.sum((total * total * counted).reshape(strip // 8, 8, width), axis=0)
+            return mixed.astype(BF16)
+
+        def first_back(at, own, total):
+            r1 = cols[at, R_ONE : R_ONE + 1]
+            unit = tok[at, :].astype(F32) * r1
+            scaled = total * gain[0:1, :]
+            mean = jnp.mean(scaled * unit, axis=-1, keepdims=True)
+            return (r.branch[at, :].astype(F32) + r1 * (scaled - unit * mean)).astype(BF16)
+
+        two = LineSum(n, strip, hop, p_two, r.left, r.right, r.branch, *g.two, second_back)
+        feed = LineSum(n, strip, hop, p_feed, gathered, r.wo, xn, *g.feed, forward)
+        one = LineSum(n, strip, hop, cot, r.left, r.right, p_two, *g.one, first_back)
+        parts = [wg, wu, wd]
+        gffn = GradSum(fsdp, ctx, parts, [1, 1, 1], None,
+                       [g.held[3 * a : 3 * a + 3] for a in range(3)], *g.gffn)
+        aparts = g.parts
+        gatt = GradSum(fsdp, ctx, aparts, axes, None,
+                       [g.held[3 * a : 3 * a + 3] for a in range(3, 8)], *g.gatt)
+
+        def block_of_rows(b):
+            at = pl.ds(pl.multiple_of(b * TILE, TILE), TILE)
+            seq = b * TILE // tok_dev
+
+            def steps(j):
+                line.step(s1 + b * per_block + j)
+                two.step((b - 1) * per_block + j)
+
+            branch = dot(gathered[at, :], r.wo[...])
+            middle_rows = tok[at, :].astype(F32) + branch
+            mid[at, :] = middle_rows
+            r.sacc[2 * seq_dev + seq] += jnp.sum(
+                (branch * branch * cols[at, VALID : VALID + 1]).reshape(TILE // 8, 8, width), axis=0
+            )
+            level = lax.rsqrt(jnp.mean(middle_rows * middle_rows, axis=-1, keepdims=True) + eps)
+            cols[at, R_TWO : R_TWO + 1] = level
+            unit = (middle_rows * level * gain[1:2, :]).astype(BF16)
+            xn[at, :] = unit
+            steps(0)
+            gate = dot_t(unit, wg[...])
+            upper = dot_t(unit, wu[...])
+            sigma = jax.nn.sigmoid(gate)
+            swish = gate * sigma
+            hidden = (swish * upper).astype(BF16)
+            r.hid[at, :] = hidden
+            slope = upper * sigma * (1.0 + gate * (1.0 - sigma))
+            steps(1)
+            p_feed[at, :] = dot(hidden, wd[...]).astype(BF16)
+            d_hidden = dot_t(cot[at, :], wd[...])
+            d_gate = (d_hidden * slope).astype(BF16)
+            d_upper = (d_hidden * swish).astype(BF16)
+            r.dg[at, :] = d_gate
+            r.du[at, :] = d_upper
+            steps(2)
+            p_two[at, :] = (dot(d_gate, wg[...]) + dot(d_upper, wu[...])).astype(BF16)
+            steps(3)
+
+        loop(0, q_tiles, block_of_rows)
+        s2 = (q_tiles - 1) * per_block
+
+        def product(i):
+            at = pl.ds(pl.multiple_of(i * cols_at, cols_at), cols_at)
+            left = xn[:, at]
+            parts[0][:, at] = dot_rows(r.dg[...], left).astype(BF16)
+            parts[1][:, at] = dot_rows(r.du[...], left).astype(BF16)
+            parts[2][:, at] = dot_rows(r.hid[...], cot[:, at]).astype(BF16)
+
+        def busy(s):
+            two.step(s)
+            product(s - s2)
+
+        line.drain()
+        loop(s2, s2 + 4, busy)
+        gffn.start()
+        s2 = s2 + 4
+
+        dk, dv, dqb, grad_seq, lat_parts = r.dk, r.dv, r.dqb, r.grad_seq, r.lat_parts
+
+        def clear(i):
+            at = pl.ds(pl.multiple_of(i * TILE, TILE), TILE)
+            dk[at, :] = jnp.zeros((TILE, q_width), F32)
+            dv[at, :] = jnp.zeros((TILE, q_width), F32)
+
+        loop(0, keyed // TILE, clear)
+        ready = steps_all // seq_dev + lag
+        loop(s2, ready, two.step)
+
+        def grad_tile(i, step):
+            seq = i // per
+            q_tile = own_shard * per + lax.rem(i, per)
+            at = pl.ds(pl.multiple_of(i * TILE, TILE), TILE)
+            near = pl.ds(pl.multiple_of((seq * win * per + q_tile - span) * TILE, TILE), tiles * TILE)
+            grad_seq[...] = dot_t(r.branch[at, :], r.wo_rows[...]).astype(BF16)
+            inner_sum = grad_seq[...].astype(F32) * att[at, :].astype(F32)
+            counted = jnp.concatenate(
+                [
+                    c.astype(F32)
+                    for c in counted_keys(cols, segk, at, seq, q_tile * TILE, q_tile - span, tiles, tok_dev, win)
+                ],
+                axis=1,
+            )
+            d_query = jnp.zeros((TILE, q_width), F32)
+            d_key = jnp.zeros((tiles * TILE, q_width), F32)
+            d_value = jnp.zeros((tiles * TILE, q_width), F32)
+            for h in range(heads):
+                delta = jnp.sum(head_only(inner_sum, h), axis=-1, keepdims=True)
+                asked, ours = head_only(r.query[at, :], h), head_only(grad_seq[...], h)
+                score = jnp.where(counted > 0.0, dot_t(asked, r.keys[near, :]) * 0.125, -1e30)
+                prob = jnp.exp(score - cols[at, LSE + h : LSE + h + 1]) * counted
+                d_score = (prob * (dot_t(ours, r.values[near, :]) - delta)).astype(BF16)
+                d_query = d_query + jnp.dot(d_score, head_only(r.keys[near, :], h), preferred_element_type=F32)
+                d_key = d_key + dot_rows(d_score, asked)
+                d_value = d_value + dot_rows(prob.astype(BF16), ours)
+                step(h)
+            dqb[at, :] = (d_query * 0.125).astype(BF16)
+            dk[near, :] += d_key * 0.125
+            dv[near, :] += d_value
+
+        def send_latent(seq, i):
+            j = seq * per_seq + i
+            at = pl.ds(pl.multiple_of(j * chunk, chunk), chunk)
+            return remote(lat_parts.at[place(own_shard - 1, j)], r.came.at[at], r.c_sent.at[seq, i],
+                          r.c_recv.at[seq, i], {"ctx": x - 1})
+
+        def latents(seq):
+            for shard in (own_shard - 1, own_shard):
+                for i in range(per_seq):
+                    at = place(shard, seq * per_seq + i)
+                    lat_parts[at, :] = (
+                        dot_t(dk[at, :].astype(BF16), r.w_kproj[...])
+                        + dot_t(dv[at, :].astype(BF16), r.w_vproj[...])
+                    ).astype(BF16)
+                    if shard < own_shard:
+
+                        @pl.when(x - 1 >= 0)
+                        def _(i=i):
+                            send_latent(seq, i).start()
+
+        def sequence(seq):
+            def tile(i):
+                def step(h):
+                    t = (i * heads + h) * steps_per // heads
+                    two.step(ready + t)
+                    feed.step(t)
+
+                grad_tile(i, step)
+
+            loop(seq * per, seq * per + per, tile)
+            latents(seq)
+
+            @pl.when(seq == 0)
+            def _():
+                two.drain()
+                gffn.pair()
+
+            @pl.when(seq == seq_dev - 1)
+            def _():
+                gffn.second()
+
+        steps_per = heads
+        loop(0, seq_dev, sequence)
+        fed = q_tiles * steps_per
+
+        def whole_latent(j):
+            seq, i = j // per_seq, lax.rem(j, per_seq)
+            at = pl.ds(pl.multiple_of(j * chunk, chunk), chunk)
+            r.dlat[at, :] = lat_parts[place(own_shard, j), :]
+
+            @pl.when(x + 1 < ctx)
+            def _():
+                wait_came(r.came.at[at], r.c_sent.at[seq, i], r.c_recv.at[seq, i])
+                r.dlat[at, :] = (r.dlat[at, :].astype(F32) + r.came[at, :].astype(F32)).astype(BF16)
+
+            cot[at, :] = (dot_t(dqb[at, :], r.w_qry[...]) + dot_t(r.dlat[at, :], r.w_lat[...])).astype(BF16)
+
+        def steps(s):
+            one.step(s)
+            feed.step(fed + s)
+
+        def first_unit_columns(at):
+            return (tok[:, at].astype(F32) * cols[:, R_ONE : R_ONE + 1] * gain[0:1, at]).astype(BF16)
+
+        early = (seq_dev - 1) * per_seq
+        loop(0, early, whole_latent)
+
+        def mixed_work(i):
+            at = pl.ds(pl.multiple_of(i * chunk, chunk), chunk)
+            aparts[0][at, :] = dot_rows(first_unit_columns(at), dqb[...]).astype(BF16)
+            aparts[3][:, at] = dot_rows(att[...], r.branch[:, at]).astype(BF16)
+            steps(i)
+
+        s0 = width // chunk
+        loop(0, s0, mixed_work)
+        loop(early, pieces, whole_latent)
+        aparts[1][...] = dot_rows(lat_all[...], dk[...].astype(BF16)).astype(BF16)
+        steps(s0)
+        aparts[2][...] = dot_rows(lat_all[...], dv[...].astype(BF16)).astype(BF16)
+        steps(s0 + 1)
+        s0 = s0 + 2
+
+        def product_lat(s):
+            at = pl.ds(pl.multiple_of((s - s0) * chunk, chunk), chunk)
+            aparts[4][at, :] = dot_rows(first_unit_columns(at), r.dlat[...]).astype(BF16)
+            steps(s)
+
+        begun = s0 + width // chunk
+        loop(s0, begun, product_lat)
+        gatt.start()
+        gffn.third()
+
+        def gains_of(i):
+            at = pl.ds(pl.multiple_of(i * side, side), side)
+            value = cot[at, :].astype(F32) * (tok[at, :].astype(F32) * cols[at, R_ONE : R_ONE + 1])
+            r.g_sum[...] += jnp.sum(value.reshape(side // 8, 8, width), axis=0)
+            along = lax.dot_general(jnp.ones((8, width), F32), value * gain[0:1, :], (((1,), (1,)), ((), ())),
+                                    precision=lax.Precision.HIGHEST, preferred_element_type=F32)
+            r.sm[3:4, at] = along[0:1, :]
+            lines = cols[at, :].T
+            r.sm[4:5, at] = lines[MARK : MARK + 1, :]
+            r.sm[5:6, at] = lines[R_ONE : R_ONE + 1, :]
+
+        def two_gains(s):
+            steps(s)
+            gains_of(2 * (s - begun))
+            gains_of(2 * (s - begun) + 1)
+
+        mark = begun + rows // side // 2
+        loop(begun, begun + 1, two_gains)
+        gatt.pair()
+        gatt.second()
+        loop(begun + 1, mark, two_gains)
+        last = one.steps()
+        for s in range(fed + mark, feed.steps()):
+            feed.step(s)
+        flush = r.flush
+        out_mixed = pltpu.make_async_copy(xn, o_mixed, flush.at[8])
+        out_mixed.start()
+        gatt.third()
+        lane = lax.broadcasted_iota(jnp.int32, (1, many), 1)
+        once = jnp.where(me == 0, 1.0, 0.0)
+        row = jnp.zeros((1, many), F32)
+
+        def whole_sum(value):
+            return jnp.sum(jnp.sum(value, axis=0, keepdims=True), axis=1, keepdims=True)
+
+        for q in range(seq_dev):
+            stats = [
+                whole_sum(r.sacc[q]),
+                whole_sum(r.sacc[seq_dev + q]),
+                whole_sum(r.sacc[2 * seq_dev + q]) * once,
+                jnp.sum(cols[q * tok_dev : (q + 1) * tok_dev, VALID : VALID + 1], axis=0, keepdims=True) * once,
+            ]
+            for j, value in enumerate(stats):
+                row = row + jnp.where(lane == 4 * q + j, value, 0.0)
+        r.sm[2:3, :] = row
+        r.sm[0:1, 0:width] = jnp.sum(r.g_sum[...], axis=0, keepdims=True)
+        r.sm[1:2, 0:width] = jnp.sum(r.g_sum2[...], axis=0, keepdims=True)
+        r_row = r.sm[5:6, :]
+        over_tp = AxisSum("tp", n, *g.s_tp)
+        over_ctx = AxisSum("ctx", ctx, *g.s_ctx)
+        over_fsdp = AxisSum("fsdp", fsdp, *g.s_fsdp)
+        over_tp.start(r.sm[...])
+        lline = RowGather(n, r.lat_own, r.lat_every, *g.lline)
+        outward = Bring([(outs[i], o_blocks[i]) for i in range(8)], flush)
+
+        def store(a, at, total):
+            if a < 4:
+                outs[a][at, :] = total
+            else:
+                r.lat_own[at, :] = total.astype(BF16)
+
+        def store_ffn(a, at, total):
+            outs[5 + a][at, :] = total
+
+        loop(mark, mark + 2, steps)
+        along_tp = over_tp.finish()
+        over_ctx.start(along_tp)
+        gffn.fourth(store_ffn)
+        outward.start([5, 6, 7])
+        loop(mark + 2, mark + 4, steps)
+        gatt.fourth(store)
+        outward.start([0, 1, 2, 3])
+        lline.start()
+        along_ctx = over_ctx.finish()
+        over_fsdp.start(along_ctx)
+        loop(mark + 4, mark + 6, steps)
+        lline.relay([1])
+        everywhere = over_fsdp.finish()
+        loop(mark + 6, mark + 8, steps)
+        if n > 2:
+            lline.relay([2])
+        loop(mark + 8, last, steps)
+        if n > 3:
+            lline.relay(range(3, n))
+        out_tok = pltpu.make_async_copy(p_two, o_tok, flush.at[9])
+        out_tok.start()
+        row = lax.broadcasted_iota(jnp.int32, everywhere.shape, 0)
+        o_small[...] = jnp.where(row < 2, everywhere, along_ctx)
+        o_small[3:4, :] = (along_tp[4:5] + eps * r_row * r_row * r_row * along_tp[3:4]) * (1.0 / width**0.5)
+        lline.finish()
+
+        def latent_sum(i):
+            at = pl.ds(pl.multiple_of(i * 16, 16), 16)
+            for gr in range(GROUPS):
+                total = jnp.zeros((16, lat[1]), F32)
+                for t in range(n):
+                    if t * GROUPS // n == gr:
+                        total = total + r.lat_every[t, at, :].astype(F32)
+                outs[4][at, gr * lat[1] : (gr + 1) * lat[1]] = total
+
+        loop(0, lat[0] // 16, latent_sum)
+        outward.start([4])
+
+        @pl.when(x + 1 < ctx)
+        def _():
+            loop(0, pieces, lambda i: pass_on(i).wait_send())
+
+        @pl.when(x - 1 >= 0)
+        def _():
+            for seq in range(seq_dev):
+                for i in range(per_seq):
+                    send_latent(seq, i).wait_send()
+
+        feed.drain()
+        one.drain()
+        gffn.drain_pair()
+        gffn.drain()
+        gatt.drain_pair()
+        gatt.drain()
+        outward.wait()
+        out_mixed.wait()
+        out_tok.wait()
+
+    out = pl.pallas_call(
+        kernel,
+        out_shape=(shape_of((rows, width), BF16),) * 2 + tuple(out_blocks) + (shape_of((8, many), F32),),
+        in_specs=[ANY] + [VMEM] * 2 + [ANY] * 8 + [VMEM, ANY],
+        out_specs=(ANY,) * 10 + (VMEM,),
+        scratch_shapes=shapes,
+        compiler_params=params(1, 64),
+    )(tokens, gain1, gain2, w_latent, *shards, w_out, *wide_shards, segments, out_grad)
+    return out[0], out[1], out[2:7], out[7:10], out[10]
+
+
+def three_kernels(tokens, gain1, gain2, w_latent, shards, w_out, wide_shards, segments, out_grad, fsdp, ctx, n):
+    seq_dev, tok_dev = segments.shape
+    gate, up, down = wide_shards
+    (xn_one, cols, gains, w_lat, w_qry, w_kproj, w_vproj, gate_all, up_all, wo_cols, seg_all, lat_all,
+     query, keys, values) = front(tokens, gain1, gain2, w_latent, shards, w_out, (gate, up), segments, fsdp, ctx, n)
+    late = window(ctx, tok_dev) <= 2
+    (d_branch, part_feed, d_middle, mid_own, wo_rows, gain_part, branch_sq, marks, attended, lse), ffn = middle(
+        query, keys, values, seg_all, cols, (wo_cols.reshape(-1, w_out.shape[1]), down), gate_all, up_all, gains,
+        tokens, out_grad, fsdp, ctx, n, seq_dev, late,
+    )
+    (grad_tokens, mixed, small), att_grads, late_ffn = back(
+        query, keys, values, seg_all, cols, lse, attended, d_branch, wo_rows, (w_qry, w_lat, w_kproj, w_vproj),
+        lat_all, xn_one, gains, tokens, d_middle, mid_own, part_feed, marks, gain_part, branch_sq,
+        ffn if late else (), fsdp, ctx, n, seq_dev,
+    )
+    return mixed, grad_tokens, att_grads, late_ffn if late else ffn, small
+
+
 def on_device(
     tokens, gain1, w_latent, w_query, w_key, w_value, w_out, gain2, w_gate, w_up, w_down, segments, cotangent
 ):
@@ -1450,27 +2180,20 @@
     row_count = seq_dev * tok_dev
     tok_rows = tokens.reshape(row_count, feat_dim)
     out_grad = cotangent.reshape(row_count, feat_dim)
-    (xn_one, cols, gains, w_lat, w_qry, w_kproj, w_vproj, gate_all, up_all, wo_cols, seg_all, lat_all,
-     query, keys, values) = front(
-        tok_rows, gain1, gain2, w_latent, (w_query, w_key, w_value), w_out, (w_gate.T, w_up.T), segments,
-        n_fsdp, n_ctx, n_tp,
+    if n_ctx == 2 and n_fsdp >= 4 and w_down.shape[0] <= row_count and feat_dim <= row_count:
+        mixed, grad_tokens, att_grads, ffn_grads, small = layer(
+            tok_rows, gain1, gain2, w_latent, (w_query, w_key, w_value), w_out, (w_gate.T, w_up.T, w_down), segments,
+            out_grad, n_fsdp, n_ctx, n_tp,
+        )
+    else:
+        mixed, grad_tokens, att_grads, ffn_grads, small = three_kernels(
+            tok_rows, gain1, gain2, w_latent, (w_query, w_key, w_value), w_out, (w_gate.T, w_up.T, w_down), segments,
+            out_grad, n_fsdp, n_ctx, n_tp,
+        )
+    arrays, gain_grads, stats, radial = publish(
+        (mixed, grad_tokens, *att_grads, *ffn_grads), small, seq_dev, tok_dev, feat_dim, n_fsdp
     )
-    late = window(n_ctx, tok_dev) <= 2
-    (d_branch, part_feed, d_middle, mid_own, wo_rows, gain_part, branch_sq, marks, attended, lse), ffn = middle(
-        query, keys, values, seg_all, cols, (wo_cols.reshape(-1, w_out.shape[1]), w_down), gate_all, up_all, gains,
-        tok_rows, out_grad, n_fsdp, n_ctx, n_tp, seq_dev, late,
-    )
-    (grad_tokens, mixed, small), (s_qry, s_kproj, s_vproj, s_outp, s_lat), late_ffn = back(
-        query, keys, values, seg_all, cols, lse, attended, d_branch, wo_rows, (w_qry, w_lat, w_kproj, w_vproj),
-        lat_all, xn_one, gains, tok_rows, d_middle, mid_own, part_feed, marks, gain_part, branch_sq,
-        ffn if late else (), n_fsdp, n_ctx, n_tp, seq_dev,
-    )
-    s_gate, s_up, s_down = late_ffn if late else ffn
-    arrays, gain_grads, stats, radial = publish(
-        (mixed, grad_tokens, s_lat, s_qry, s_kproj, s_vproj, s_outp, s_gate, s_up, s_down), small,
-        seq_dev, tok_dev, feat_dim, n_fsdp,
-    )
-    mixed, grad_tokens, s_lat, s_qry, s_kproj, s_vproj, s_outp, s_gate, s_up, s_down = arrays
+    mixed, grad_tokens, s_qry, s_kproj, s_vproj, s_outp, s_lat, s_gate, s_up, s_down = arrays
     return (
         mixed.reshape(seq_dev, tok_dev, feat_dim),
         grad_tokens.reshape(seq_dev, tok_dev, feat_dim),

time: 289 us -> 246 us (0.85)
  Pallas kernels: 287 us -> 243 us
    pallas_call x3 -> x1, Pallas kernels: 280 us -> 236 us  [layer(): pl.pallas_call(kernel, out_shape=(shape_of((rows, width), BF16),) * 2 + t...]
where the time goes in v1:
time: 246 us; the launch traced here: 245 us
  Pallas kernels  243 us (99%)
    pallas_call x1, Pallas kernels, layer(): pl.pallas_call(kernel, out_shape=(shape_of((rows, width), BF16),) * 2 + t...  236 us
    pallas_call x1, Pallas kernels, publish(): pl.pallas_call(kernel, out_shape=tuple((shape_of(a.shape, a.dtype) for a...  7.11 us

profile of v1, /device:TPU:0, one launch (start us, length us, event | category | flops | bytes accessed | tf_op | source)
XLA Modules:
  0.0 245.4 jit_solution(8818137927970577351)
XLA Ops:
  0.7 236.3 %shard_map.236 = (bf16[1024,1024]{1,0:T(8,128)(2,1)}, bf16[1024,1024]{1,0:T(8,128)(2,1)}, f32[256,256]{1,0:T(8,128)}, f32[64,256]{1,0:T(8,128)}, f32[64,256]{1,0...) custom-call(bf16[1024,1024]{1,0:T(8,128)(2,1)} %bitcast.10, ...), custom_call_target="tpu_custom_call" | custom-call | tf_op jit(solution)/shard_map/pallas_call | solution.py:2146
  237.0 7.1 %shard_map.237 = (bf16[1024,1024]{1,0:T(8,128)(2,1)}, bf16[1024,1024]{1,0:T(8,128)(2,1)}, f32[256,256]{1,0:T(8,128)}, f32[64,256]{1,0:T(8,128)}, f32[64,256]{1,0...) custom-call(bf16[1024,1024]{1,0:T(8,128)(2,1)} %get-tuple-element.38, ...), custom_call_target="tpu_custom_call" | custom-call | tf_op jit(solution)/shard_map/pallas_call | solution.py:1435
  244.1 1.3 fusion

commit v2 on v1

--- a/solution.py
+++ b/solution.py
@@ -279,6 +279,9 @@
     def steps(self):
         return self.count + self.hop * 2 * (self.n // 2)
 
+    def turn(self, at):
+        return lax.rem(at, self.recv.shape[2])
+
     def rows(self, slot, at):
         return pl.ds(pl.multiple_of((at * 2 + slot) * self.chunk, self.chunk), self.chunk)
 
@@ -299,17 +302,17 @@
                 def _(at=at, held=held, to=to, side=side, slot=slot):
                     rows = self.rows(slot, at)
                     remote(self.part.at[rows], held.at[rows], self.sent.at[0],
-                           self.recv.at[side, slot, at], to).start()
+                           self.recv.at[side, slot, self.turn(at)], to).start()
 
                 if n > 2:
 
                     @pl.when(here & (lag > 0))
                     def _(at=at, held=held, to=to, side=side, slot=slot):
                         rows = self.rows(slot, at)
-                        wait_came(held.at[rows], self.sent.at[0], self.recv.at[side, slot, at])
+                        wait_came(held.at[rows], self.sent.at[0], self.recv.at[side, slot, self.turn(at)])
                         held[rows, :] = (held[rows, :].astype(F32) + self.part[rows, :].astype(F32)).astype(BF16)
                         remote(held.at[rows], held.at[rows], self.sent.at[0],
-                               self.recv.at[side, slot, at], to).start()
+                               self.recv.at[side, slot, self.turn(at)], to).start()
 
             at = s - hop * reach
 
@@ -318,17 +321,17 @@
                 rows = self.rows(slot, at)
                 total = self.part[rows, :].astype(F32)
                 if owner > 0:
-                    wait_came(self.from_left.at[rows], self.sent.at[0], self.recv.at[0, slot, at])
+                    wait_came(self.from_left.at[rows], self.sent.at[0], self.recv.at[0, slot, self.turn(at)])
                     total = total + self.from_left[rows, :].astype(F32)
-                wait_came(self.from_right.at[rows], self.sent.at[0], self.recv.at[1, slot, at])
+                wait_came(self.from_right.at[rows], self.sent.at[0], self.recv.at[1, slot, self.turn(at)])
                 total = total + self.from_right[rows, :].astype(F32)
                 own = pl.ds(pl.multiple_of(at * self.chunk, self.chunk), self.chunk)
                 self.out[rows, :] = self.finish(rows, own, total)
                 if owner > 0:
                     remote(self.out.at[rows], self.out.at[rows], self.sent.at[1],
-                           self.recv.at[2, slot, at], left).start()
+                           self.recv.at[2, slot, self.turn(at)], left).start()
                 remote(self.out.at[rows], self.out.at[rows], self.sent.at[2],
-                       self.recv.at[2, slot, at], right).start()
+                       self.recv.at[2, slot, self.turn(at)], right).start()
 
         for slot, owner in enumerate(self.owners):
             away = jnp.abs(me - owner)
@@ -338,15 +341,15 @@
             def _(at=at, slot=slot, owner=owner):
                 rows = self.rows(slot, at)
                 here = self.out.at[rows]
-                wait_came(here, self.sent.at[3], self.recv.at[2, slot, at])
+                wait_came(here, self.sent.at[3], self.recv.at[2, slot, self.turn(at)])
 
                 @pl.when((me < owner) & (me > 0))
                 def _():
-                    remote(here, here, self.sent.at[3], self.recv.at[2, slot, at], left).start()
+                    remote(here, here, self.sent.at[3], self.recv.at[2, slot, self.turn(at)], left).start()
 
                 @pl.when((me > owner) & (me < n - 1))
                 def _():
-                    remote(here, here, self.sent.at[3], self.recv.at[2, slot, at], right).start()
+                    remote(here, here, self.sent.at[3], self.recv.at[2, slot, self.turn(at)], right).start()
 
     def drain(self):
         n, me, half = self.n, self.me, self.total_rows // 2
@@ -389,7 +392,7 @@
         return [
             pltpu.VMEM((rows, width), BF16),
             pltpu.VMEM((rows, width), BF16),
-            pltpu.SemaphoreType.DMA((3, 2, rows // 2 // chunk)),
+            pltpu.SemaphoreType.DMA((3, 2, min(rows // 2 // chunk, 12))),
             pltpu.SemaphoreType.DMA((4,)),
         ]
 
@@ -1416,12 +1419,14 @@
 
     def kernel(*refs):
         srcs, sm, refs = refs[:count], refs[count], refs[count + 1 :]
-        dsts, (gains, stats, radial), refs = refs[:count], refs[count : count + 3], refs[count + 3 :]
+        dsts, (gain1, gain2, stats, radial), refs = refs[:count], refs[count : count + 4], refs[count + 4 :]
         inward = Bring(list(zip(srcs, refs[:count])), refs[count])
         outward = Bring(list(zip(refs[:count], dsts)), refs[count + 1])
         inward.start()
         f = lax.axis_index("fsdp")
-        gains[...] = sm[0:2, pl.ds(pl.multiple_of(f * per, per), per)]
+        mine = pl.ds(pl.multiple_of(f * per, per), per)
+        gain1[...] = sm[0:1, mine].reshape(per)
+        gain2[...] = sm[1:2, mine].reshape(per)
         for q in range(seq_dev):
             radial[q : q + 1, :] = sm[3:4, q * tok_dev : (q + 1) * tok_dev]
             total = sm[2:3, 4 * q + 3 : 4 * q + 4] * feat_dim
@@ -1435,13 +1440,38 @@
     out = pl.pallas_call(
         kernel,
         out_shape=tuple(shape_of(a.shape, a.dtype) for a in arrays)
-        + (shape_of((2, per), F32), shape_of((seq_dev, 3), F32), shape_of((seq_dev, tok_dev), F32)),
+        + (shape_of((per,), F32),) * 2
+        + (shape_of((seq_dev, 3), F32), shape_of((seq_dev, tok_dev), F32)),
         in_specs=[ANY] * count + [VMEM],
-        out_specs=(ANY,) * count + (VMEM,) * 3,
+        out_specs=(ANY,) * count + (VMEM,) * 4,
         scratch_shapes=[pltpu.VMEM(a.shape, a.dtype) for a in arrays] + [pltpu.SemaphoreType.DMA((count,))] * 2,
         compiler_params=pltpu.CompilerParams(vmem_limit_bytes=60 << 20),
     )(*arrays, small)
-    return out[:count], out[count], out[count + 1], out[count + 2]
+    return out[:count], out[count:]
+
+
+class AxisShare:
+    def __init__(self, axis, n, src, dst, recv, sent, own):
+        self.axis, self.n, self.src, self.dst = axis, n, src, dst
+        self.recv, self.sent, self.own = recv, sent, own
+        self.at = lax.axis_index(axis)
+
+    def start(self):
+        for k in range(1, self.n):
+            remote(self.src, self.dst.at[self.at], self.sent.at[k - 1], self.recv.at[self.at],
+                   {self.axis: lax.rem(self.at + k, self.n)}).start()
+        pltpu.make_async_copy(self.src, self.dst.at[self.at], self.own).start()
+
+    def finish(self):
+        for k in range(1, self.n):
+            other = lax.rem(self.at + k, self.n)
+            wait_came(self.dst.at[other], self.sent.at[k - 1], self.recv.at[other])
+            wait_sent(self.src, self.sent.at[k - 1], self.recv.at[other])
+        pltpu.make_async_copy(self.src, self.dst.at[self.at], self.own).wait()
+
+    @staticmethod
+    def scratch(n):
+        return CtxShare.scratch(n)
 
 
 class HalfSpread:
@@ -1465,7 +1495,7 @@
     def start(self, which):
         for a in which:
             for k in range(1, self.ys):
-                remote(self.part(a), self.view(a, self.f, self.x), self.sent.at[a, 0, k], self.recv.at[a, 0, k],
+                remote(self.part(a), self.view(a, self.f, self.x), self.sent.at[a, 0, k - 1], self.recv.at[a, 0, k - 1],
                        {"fsdp": lax.rem(self.f + 2 * k, self.fsdp)}).start()
         for a in which:
             src = self.pairs[a][0]
@@ -1480,17 +1510,17 @@
         for a in which:
             for k in range(1, self.ys):
                 here = self.view(a, self.source(k), self.x)
-                wait_came(here, self.sent.at[a, 0, k], self.recv.at[a, 0, k])
-                remote(here, here, self.sent.at[a, 2, k], self.recv.at[a, 2, k], {"ctx": 1 - self.x}).start()
-                remote(here, here, self.sent.at[a, 3, k], self.recv.at[a, 3, k],
+                wait_came(here, self.sent.at[a, 0, k - 1], self.recv.at[a, 0, k - 1])
+                remote(here, here, self.sent.at[a, 2, k - 1], self.recv.at[a, 2, k - 1], {"ctx": 1 - self.x}).start()
+                remote(here, here, self.sent.at[a, 3, k - 1], self.recv.at[a, 3, k - 1],
                        {"fsdp": sibling(self.f)}).start()
 
     def cross(self, which):
         for a in which:
             for k in range(1, self.ys):
                 here = self.view(a, self.source(k), 1 - self.x)
-                wait_came(here, self.sent.at[a, 2, k], self.recv.at[a, 2, k])
-                remote(here, here, self.sent.at[a, 4, k], self.recv.at[a, 4, k],
+                wait_came(here, self.sent.at[a, 2, k - 1], self.recv.at[a, 2, k - 1])
+                remote(here, here, self.sent.at[a, 4, k - 1], self.recv.at[a, 4, k - 1],
                        {"fsdp": sibling(self.f)}).start()
 
     def finish(self, which):
@@ -1501,21 +1531,21 @@
             pltpu.make_async_copy(src, self.view(a, self.f), self.own.at[a]).wait()
             for k in range(1, self.ys):
                 there = lax.rem(other - 2 * k + self.fsdp, self.fsdp)
-                wait_came(self.view(a, there, self.x), self.sent.at[a, 3, k], self.recv.at[a, 3, k])
-                wait_came(self.view(a, there, 1 - self.x), self.sent.at[a, 4, k], self.recv.at[a, 4, k])
+                wait_came(self.view(a, there, self.x), self.sent.at[a, 3, k - 1], self.recv.at[a, 3, k - 1])
+                wait_came(self.view(a, there, 1 - self.x), self.sent.at[a, 4, k - 1], self.recv.at[a, 4, k - 1])
 
     def drain(self, which):
         for a in which:
             wait_sent(self.view(a, self.f), self.sent.at[a, 1, 0], self.recv.at[a, 1, 0])
             for k in range(1, self.ys):
                 for kind in (0, 2, 3, 4):
-                    wait_sent(self.part(a), self.sent.at[a, kind, k], self.recv.at[a, kind, k])
+                    wait_sent(self.part(a), self.sent.at[a, kind, k - 1], self.recv.at[a, kind, k - 1])
 
     @staticmethod
     def scratch(fsdp, arrays):
         return [
-            pltpu.SemaphoreType.DMA((arrays, 5, fsdp // 2)),
-            pltpu.SemaphoreType.DMA((arrays, 5, fsdp // 2)),
+            pltpu.SemaphoreType.DMA((arrays, 5, max(fsdp // 2 - 1, 1))),
+            pltpu.SemaphoreType.DMA((arrays, 5, max(fsdp // 2 - 1, 1))),
             pltpu.SemaphoreType.DMA((arrays,)),
         ]
 
@@ -1599,7 +1629,9 @@
         sm=pltpu.VMEM((8, many), F32),
         sacc=pltpu.VMEM((3 * seq_dev, 8, width), F32),
         lat_own=pltpu.VMEM(lat, BF16),
-        lat_every=pltpu.VMEM((n,) + lat, BF16),
+        lat_every=pltpu.VMEM((n, lat[0] // 2, lat[1]), BF16),
+        lat_sum=pltpu.VMEM((lat[0] // 2, GROUPS * lat[1]), BF16),
+        lat_both=pltpu.VMEM((ctx, lat[0] // 2, GROUPS * lat[1]), BF16),
         local=pltpu.SemaphoreType.DMA((2,)),
         flush=pltpu.SemaphoreType.DMA((10,)),
         lat_recv=pltpu.SemaphoreType.DMA((pieces,)),
@@ -1616,14 +1648,14 @@
         spread=Spread.scratch(fsdp, 5),
         half=HalfSpread.scratch(fsdp, 4),
         share=CtxShare.scratch(ctx),
-        wline=RowGather.scratch(n),
+        wline=AxisShare.scratch(n),
         gather=LineGather.scratch(n, rows // piece),
         two=LineSum.scratch(n, rows, width, strip)[2:],
         feed=LineSum.scratch(n, rows, width, strip)[2:],
-        one=LineSum.scratch(n, rows, width, strip)[2:],
         gffn=GradSum.semaphores(fsdp, ctx, 3),
         gatt=GradSum.semaphores(fsdp, ctx, 5),
-        lline=RowGather.scratch(n),
+        lline=AxisShare.scratch(n),
+        xline=AxisShare.scratch(ctx),
         s_tp=AxisSum.scratch(n, (8, many)),
         s_ctx=AxisSum.scratch(ctx, (8, many)),
         s_fsdp=AxisSum.scratch(fsdp, (8, many)),
@@ -1662,7 +1694,7 @@
             [1, 0, 0, 0, 0], *g.spread,
         )
         share = CtxShare(ctx, r.sbuf, segk, *g.share)
-        wline = RowGather(n, wout, r.wo_line, *g.wline)
+        wline = AxisShare("tp", n, wout, r.wo_line, *g.wline)
         half = HalfSpread(
             fsdp,
             [(wgt, r.wg), (wut, r.wu), (wdn, r.wd), (r.wo_line.reshape(n * q_width, w_out.shape[1]), r.wo)],
@@ -1708,7 +1740,6 @@
                 pass_on(i).start()
 
         loop(0, pieces, first_norm)
-        wline.relay([1])
         spread.relay([2, 3, 4])
         spread.finish([2, 3, 4])
 
@@ -1724,8 +1755,6 @@
             project(own_shard, i)
 
         loop(0, pieces, ask)
-        if n > 2:
-            wline.relay([2])
         share.finish()
         for q in range(seq_dev):
             at = slice(q * tok_dev, (q + 1) * tok_dev)
@@ -1733,10 +1762,6 @@
             cols[at, SEGMENT : SEGMENT + 1] = ids[:, 0:1]
             final = segk[ctx - 1, q : q + 1, tok_dev - 1 : tok_dev].astype(F32)
             cols[at, VALID : VALID + 1] = jnp.where(ids[:, 0:1] != final, 1.0, 0.0)
-        if n > 3:
-            wline.relay(range(3, n))
-        wline.finish()
-        half.start([3])
         half.relay([0, 1])
 
         def theirs(i):
@@ -1749,8 +1774,6 @@
                 lat_all[place(own_shard - 1, i), :] = jnp.zeros((chunk, latent), BF16)
 
             project(own_shard - 1, i)
-
-        loop(0, pieces, theirs)
 
         att, gathered = r.att, r.gathered
         line = LineGather(n, piece, att, gathered, *g.gather, hop=reach)
@@ -1780,10 +1803,23 @@
                 line.step((i - 1) * per_block + h * per_block // heads)
             att[at, :] = accum.astype(BF16)
 
-        loop(0, q_tiles, query_tile)
+        def sequence_forward(seq):
+            loop(seq * per_seq, seq * per_seq + per_seq, theirs)
+
+            @pl.when(seq == 0)
+            def _():
+                wline.finish()
+                half.start([3])
+
+            loop(seq * per, seq * per + per, query_tile)
+
+            @pl.when(seq == 0)
+            def _():
+                half.relay([2, 3])
+
+        loop(0, seq_dev, sequence_forward)
         s1 = (q_tiles - 1) * per_block
         line.begin()
-        half.relay([2, 3])
         half.cross([0, 1, 2, 3])
         loop(s1, per_block + reach * (n - 1), line.step)
         s1 = per_block + reach * (n - 1)
@@ -1822,7 +1858,7 @@
 
         two = LineSum(n, strip, hop, p_two, r.left, r.right, r.branch, *g.two, second_back)
         feed = LineSum(n, strip, hop, p_feed, gathered, r.wo, xn, *g.feed, forward)
-        one = LineSum(n, strip, hop, cot, r.left, r.right, p_two, *g.one, first_back)
+        one = LineSum(n, strip, hop, cot, r.left, r.right, p_two, *g.two, first_back)
         parts = [wg, wu, wd]
         gffn = GradSum(fsdp, ctx, parts, [1, 1, 1], None,
                        [g.held[3 * a : 3 * a + 3] for a in range(3)], *g.gffn)
@@ -1964,9 +2000,6 @@
             def _():
                 two.drain()
                 gffn.pair()
-
-            @pl.when(seq == seq_dev - 1)
-            def _():
                 gffn.second()
 
         steps_per = heads
@@ -1985,10 +2018,6 @@
 
             cot[at, :] = (dot_t(dqb[at, :], r.w_qry[...]) + dot_t(r.dlat[at, :], r.w_lat[...])).astype(BF16)
 
-        def steps(s):
-            one.step(s)
-            feed.step(fed + s)
-
         def first_unit_columns(at):
             return (tok[:, at].astype(F32) * cols[:, R_ONE : R_ONE + 1] * gain[0:1, at]).astype(BF16)
 
@@ -1999,26 +2028,27 @@
             at = pl.ds(pl.multiple_of(i * chunk, chunk), chunk)
             aparts[0][at, :] = dot_rows(first_unit_columns(at), dqb[...]).astype(BF16)
             aparts[3][:, at] = dot_rows(att[...], r.branch[:, at]).astype(BF16)
-            steps(i)
-
-        s0 = width // chunk
-        loop(0, s0, mixed_work)
+            feed.step(fed + i)
+
+        fed_later = fed + width // chunk
+        loop(0, width // chunk, mixed_work)
+        gffn.third()
+        aparts[1][...] = dot_rows(lat_all[...], dk[...].astype(BF16)).astype(BF16)
+        aparts[2][...] = dot_rows(lat_all[...], dv[...].astype(BF16)).astype(BF16)
         loop(early, pieces, whole_latent)
-        aparts[1][...] = dot_rows(lat_all[...], dk[...].astype(BF16)).astype(BF16)
-        steps(s0)
-        aparts[2][...] = dot_rows(lat_all[...], dv[...].astype(BF16)).astype(BF16)
-        steps(s0 + 1)
-        s0 = s0 + 2
+
+        def steps(s):
+            one.step(s)
+            feed.step(fed_later + s)
 
         def product_lat(s):
-            at = pl.ds(pl.multiple_of((s - s0) * chunk, chunk), chunk)
+            at = pl.ds(pl.multiple_of(s * chunk, chunk), chunk)
             aparts[4][at, :] = dot_rows(first_unit_columns(at), r.dlat[...]).astype(BF16)
             steps(s)
 
-        begun = s0 + width // chunk
-        loop(s0, begun, product_lat)
+        begun = width // chunk
+        loop(0, begun, product_lat)
         gatt.start()
-        gffn.third()
 
         def gains_of(i):
             at = pl.ds(pl.multiple_of(i * side, side), side)
@@ -2042,12 +2072,11 @@
         gatt.second()
         loop(begun + 1, mark, two_gains)
         last = one.steps()
-        for s in range(fed + mark, feed.steps()):
+        for s in range(fed_later + mark, feed.steps()):
             feed.step(s)
         flush = r.flush
         out_mixed = pltpu.make_async_copy(xn, o_mixed, flush.at[8])
         out_mixed.start()
-        gatt.third()
         lane = lax.broadcasted_iota(jnp.int32, (1, many), 1)
         once = jnp.where(me == 0, 1.0, 0.0)
         row = jnp.zeros((1, many), F32)
@@ -2072,7 +2101,9 @@
         over_ctx = AxisSum("ctx", ctx, *g.s_ctx)
         over_fsdp = AxisSum("fsdp", fsdp, *g.s_fsdp)
         over_tp.start(r.sm[...])
-        lline = RowGather(n, r.lat_own, r.lat_every, *g.lline)
+        lat_half = pl.ds(pl.multiple_of(x * (lat[0] // 2), lat[0] // 2), lat[0] // 2)
+        lline = AxisShare("tp", n, r.lat_own.at[lat_half], r.lat_every, *g.lline)
+        xline = AxisShare("ctx", ctx, r.lat_sum, r.lat_both, *g.xline)
         outward = Bring([(outs[i], o_blocks[i]) for i in range(8)], flush)
 
         def store(a, at, total):
@@ -2085,30 +2116,20 @@
             outs[5 + a][at, :] = total
 
         loop(mark, mark + 2, steps)
+        gatt.third()
         along_tp = over_tp.finish()
         over_ctx.start(along_tp)
         gffn.fourth(store_ffn)
         outward.start([5, 6, 7])
         loop(mark + 2, mark + 4, steps)
+        along_ctx = over_ctx.finish()
+        over_fsdp.start(along_ctx)
+        loop(mark + 4, mark + 6, steps)
         gatt.fourth(store)
         outward.start([0, 1, 2, 3])
         lline.start()
-        along_ctx = over_ctx.finish()
-        over_fsdp.start(along_ctx)
-        loop(mark + 4, mark + 6, steps)
-        lline.relay([1])
         everywhere = over_fsdp.finish()
-        loop(mark + 6, mark + 8, steps)
-        if n > 2:
-            lline.relay([2])
-        loop(mark + 8, last, steps)
-        if n > 3:
-            lline.relay(range(3, n))
-        out_tok = pltpu.make_async_copy(p_two, o_tok, flush.at[9])
-        out_tok.start()
-        row = lax.broadcasted_iota(jnp.int32, everywhere.shape, 0)
-        o_small[...] = jnp.where(row < 2, everywhere, along_ctx)
-        o_small[3:4, :] = (along_tp[4:5] + eps * r_row * r_row * r_row * along_tp[3:4]) * (1.0 / width**0.5)
+        loop(mark + 6, mark + 10, steps)
         lline.finish()
 
         def latent_sum(i):
@@ -2118,10 +2139,21 @@
                 for t in range(n):
                     if t * GROUPS // n == gr:
                         total = total + r.lat_every[t, at, :].astype(F32)
-                outs[4][at, gr * lat[1] : (gr + 1) * lat[1]] = total
-
-        loop(0, lat[0] // 16, latent_sum)
+                r.lat_sum[at, gr * lat[1] : (gr + 1) * lat[1]] = total.astype(BF16)
+
+        loop(0, lat[0] // 32, latent_sum)
+        xline.start()
+        loop(mark + 10, mark + 13, steps)
+        xline.finish()
+        for k in range(ctx):
+            outs[4][k * (lat[0] // 2) : (k + 1) * (lat[0] // 2), :] = r.lat_both[k].astype(F32)
         outward.start([4])
+        row = lax.broadcasted_iota(jnp.int32, everywhere.shape, 0)
+        o_small[...] = jnp.where(row < 2, everywhere, along_ctx)
+        o_small[3:4, :] = (along_tp[4:5] + eps * r_row * r_row * r_row * along_tp[3:4]) * (1.0 / width**0.5)
+        loop(mark + 13, last, steps)
+        out_tok = pltpu.make_async_copy(p_two, o_tok, flush.at[9])
+        out_tok.start()
 
         @pl.when(x + 1 < ctx)
         def _():
@@ -2190,20 +2222,20 @@
             tok_rows, gain1, gain2, w_latent, (w_query, w_key, w_value), w_out, (w_gate.T, w_up.T, w_down), segments,
             out_grad, n_fsdp, n_ctx, n_tp,
         )
-    arrays, gain_grads, stats, radial = publish(
+    arrays, (gain_grad1, gain_grad2, stats, radial) = publish(
         (mixed, grad_tokens, *att_grads, *ffn_grads), small, seq_dev, tok_dev, feat_dim, n_fsdp
     )
     mixed, grad_tokens, s_qry, s_kproj, s_vproj, s_outp, s_lat, s_gate, s_up, s_down = arrays
     return (
         mixed.reshape(seq_dev, tok_dev, feat_dim),
         grad_tokens.reshape(seq_dev, tok_dev, feat_dim),
-        gain_grads[0],
+        gain_grad1,
         s_lat,
         s_qry,
         s_kproj,
         s_vproj,
         s_outp,
-        gain_grads[1],
+        gain_grad2,
         s_gate.T,
         s_up.T,
         s_down,

time: 246 us -> 237 us (0.963)
  Pallas kernels: 243 us -> 235 us
    pallas_call x1, Pallas kernels: 236 us -> 228 us  [layer(): pl.pallas_call(kernel, out_shape=(shape_of((rows, width), BF16),) * 2 + t...]
where the time goes in v2:
time: 237 us; the launch traced here: 236 us
  Pallas kernels  235 us (99%)
    pallas_call x1, Pallas kernels, layer(): pl.pallas_call(kernel, out_shape=(shape_of((rows, width), BF16),) * 2 + t...  228 us
    pallas_call x1, Pallas kernels, publish(): pl.pallas_call(kernel, out_shape=tuple((shape_of(a.shape, a.dtype) for a...  7.12 us

profile of v2, /device:TPU:0, one launch (start us, length us, event | category | flops | bytes accessed | tf_op | source)
XLA Modules:
  0.0 236.3 jit_solution(13419005362200967348)
XLA Ops:
  0.7 228.4 %shard_map.236 = (bf16[1024,1024]{1,0:T(8,128)(2,1)}, bf16[1024,1024]{1,0:T(8,128)(2,1)}, f32[256,256]{1,0:T(8,128)}, f32[64,256]{1,0:T(8,128)}, f32[64,256]{1,0...) custom-call(bf16[1024,1024]{1,0:T(8,128)(2,1)} %bitcast.8, ...), custom_call_target="tpu_custom_call" | custom-call | tf_op jit(solution)/shard_map/pallas_call | solution.py:2178
  229.0 7.1 %shard_map.237 = (bf16[1024,1024]{1,0:T(8,128)(2,1)}, bf16[1024,1024]{1,0:T(8,128)(2,1)}, f32[256,256]{1,0:T(8,128)}, f32[64,256]{1,0:T(8,128)}, f32[64,256]{1,0...) custom-call(bf16[1024,1024]{1,0:T(8,128)(2,1)} %get-tuple-element.39, ...), custom_call_target="tpu_custom_call" | custom-call | tf_op jit(solution)/shard_map/pallas_call | solution.py:1440

commit v3 on v2

--- a/solution.py
+++ b/solution.py
@@ -266,8 +266,8 @@
 
 
 class LineSum:
-    def __init__(self, n, chunk, hop, part, from_left, from_right, out, recv, sent, finish):
-        self.n, self.chunk, self.hop = n, chunk, hop
+    def __init__(self, n, chunk, hop, part, from_left, from_right, out, recv, sent, finish, pushed=False):
+        self.n, self.chunk, self.hop, self.pushed = n, chunk, hop, pushed
         self.total_rows = part.shape[0]
         self.owners = (n // 2 - 1, n // 2)
         self.count = self.total_rows // 2 // chunk
@@ -284,6 +284,23 @@
 
     def rows(self, slot, at):
         return pl.ds(pl.multiple_of((at * 2 + slot) * self.chunk, self.chunk), self.chunk)
+
+    def send(self, here, side, slot, at):
+        held = self.from_left if side == 0 else self.from_right
+        to = {"tp": self.me + 1} if side == 0 else {"tp": self.me - 1}
+
+        @pl.when(here)
+        def _():
+            rows = self.rows(slot, at)
+            remote(self.part.at[rows], held.at[rows], self.sent.at[0], self.recv.at[side, slot, self.turn(at)],
+                   to).start()
+
+    def push(self, at):
+        for slot, owner in enumerate(self.owners):
+            if owner > 0:
+                self.send(self.me == 0, 0, slot, at)
+            if owner < self.n - 1:
+                self.send(self.me == self.n - 1, 1, slot, at)
 
     def step(self, s):
         n, me, hop = self.n, self.me, self.hop
@@ -298,11 +315,8 @@
                 to = right if side == 0 else left
                 here = here & (at >= 0) & (at < self.count)
 
-                @pl.when(here & (lag == 0))
-                def _(at=at, held=held, to=to, side=side, slot=slot):
-                    rows = self.rows(slot, at)
-                    remote(self.part.at[rows], held.at[rows], self.sent.at[0],
-                           self.recv.at[side, slot, self.turn(at)], to).start()
+                if not self.pushed:
+                    self.send(here & (lag == 0), side, slot, at)
 
                 if n > 2:
 
@@ -1568,7 +1582,7 @@
     wide, chunk = 128, 256
     pieces = rows // chunk
     per_seq = tok_dev // chunk
-    strip, hop, reach = 32, 2, 3
+    strip, hop, reach, behind = 32, 2, 3, 2
     piece = 64
     per_block = TILE // piece
     side = 128
@@ -1633,7 +1647,7 @@
         lat_sum=pltpu.VMEM((lat[0] // 2, GROUPS * lat[1]), BF16),
         lat_both=pltpu.VMEM((ctx, lat[0] // 2, GROUPS * lat[1]), BF16),
         local=pltpu.SemaphoreType.DMA((2,)),
-        flush=pltpu.SemaphoreType.DMA((10,)),
+        flush=pltpu.SemaphoreType.DMA((11,)),
         lat_recv=pltpu.SemaphoreType.DMA((pieces,)),
         lat_sent=pltpu.SemaphoreType.DMA((pieces,)),
         c_recv=pltpu.SemaphoreType.DMA((seq_dev, per_seq)),
@@ -1648,7 +1662,7 @@
         spread=Spread.scratch(fsdp, 5),
         half=HalfSpread.scratch(fsdp, 4),
         share=CtxShare.scratch(ctx),
-        wline=AxisShare.scratch(n),
+        wline=RowGather.scratch(n),
         gather=LineGather.scratch(n, rows // piece),
         two=LineSum.scratch(n, rows, width, strip)[2:],
         feed=LineSum.scratch(n, rows, width, strip)[2:],
@@ -1684,7 +1698,7 @@
         r.gbuf[1:2, :] = gb[...].astype(F32).reshape(1, -1)
         r.sbuf[...] = jnp.zeros_like(r.sbuf)
         r.sbuf[0:seq_dev, :] = seg[...]
-        meet(n, fsdp, ctx, everyone=True)
+        meet(n, fsdp, ctx)
 
         group = me * q_width // per_group
         src_lat = wlat.at[:, pl.ds(pl.multiple_of(group * latent, latent), latent)]
@@ -1694,7 +1708,7 @@
             [1, 0, 0, 0, 0], *g.spread,
         )
         share = CtxShare(ctx, r.sbuf, segk, *g.share)
-        wline = AxisShare("tp", n, wout, r.wo_line, *g.wline)
+        wline = RowGather(n, wout, r.wo_line, *g.wline)
         half = HalfSpread(
             fsdp,
             [(wgt, r.wg), (wut, r.wu), (wdn, r.wd), (r.wo_line.reshape(n * q_width, w_out.shape[1]), r.wo)],
@@ -1719,6 +1733,7 @@
         loop(0, rows // wide, scale)
         spread.relay([0, 1])
         spread.finish([0, 1])
+        wline.relay([1])
         lat_all = r.lat_all
 
         def place(shard, i):
@@ -1740,6 +1755,8 @@
                 pass_on(i).start()
 
         loop(0, pieces, first_norm)
+        if n > 2:
+            wline.relay([2])
         spread.relay([2, 3, 4])
         spread.finish([2, 3, 4])
 
@@ -1808,6 +1825,8 @@
 
             @pl.when(seq == 0)
             def _():
+                if n > 3:
+                    wline.relay(range(3, n))
                 wline.finish()
                 half.start([3])
 
@@ -1856,7 +1875,7 @@
             mean = jnp.mean(scaled * unit, axis=-1, keepdims=True)
             return (r.branch[at, :].astype(F32) + r1 * (scaled - unit * mean)).astype(BF16)
 
-        two = LineSum(n, strip, hop, p_two, r.left, r.right, r.branch, *g.two, second_back)
+        two = LineSum(n, strip, hop, p_two, r.left, r.right, r.branch, *g.two, second_back, pushed=True)
         feed = LineSum(n, strip, hop, p_feed, gathered, r.wo, xn, *g.feed, forward)
         one = LineSum(n, strip, hop, cot, r.left, r.right, p_two, *g.two, first_back)
         parts = [wg, wu, wd]
@@ -1872,7 +1891,7 @@
 
             def steps(j):
                 line.step(s1 + b * per_block + j)
-                two.step((b - 1) * per_block + j)
+                two.step((b - 1) * per_block + j - behind)
 
             branch = dot(gathered[at, :], r.wo[...])
             middle_rows = tok[at, :].astype(F32) + branch
@@ -1902,9 +1921,11 @@
             steps(2)
             p_two[at, :] = (dot(d_gate, wg[...]) + dot(d_upper, wu[...])).astype(BF16)
             steps(3)
+            for j in range(per_block):
+                two.push(b * per_block + j)
 
         loop(0, q_tiles, block_of_rows)
-        s2 = (q_tiles - 1) * per_block
+        s2 = (q_tiles - 1) * per_block - behind
 
         def product(i):
             at = pl.ds(pl.multiple_of(i * cols_at, cols_at), cols_at)
@@ -2151,9 +2172,11 @@
         row = lax.broadcasted_iota(jnp.int32, everywhere.shape, 0)
         o_small[...] = jnp.where(row < 2, everywhere, along_ctx)
         o_small[3:4, :] = (along_tp[4:5] + eps * r_row * r_row * r_row * along_tp[3:4]) * (1.0 / width**0.5)
+        ahead = [pl.ds(0, rows // 2), pl.ds(rows // 2, rows // 2)]
+        out_tok = Bring([(p_two.at[q], o_tok.at[q]) for q in ahead], flush.at[pl.ds(9, 2)])
+        out_tok.start([0])
         loop(mark + 13, last, steps)
-        out_tok = pltpu.make_async_copy(p_two, o_tok, flush.at[9])
-        out_tok.start()
+        out_tok.start([1])
 
         @pl.when(x + 1 < ctx)
         def _():

time: 237 us -> 233 us (0.983)
  Pallas kernels: 235 us -> 231 us
    pallas_call x1, Pallas kernels: 228 us -> 224 us  [layer(): pl.pallas_call(kernel, out_shape=(shape_of((rows, width), BF16),) * 2 + t...]
where the time goes in v3:
time: 233 us; the launch traced here: 232 us
  Pallas kernels  231 us (99%)
    pallas_call x1, Pallas kernels, layer(): pl.pallas_call(kernel, out_shape=(shape_of((rows, width), BF16),) * 2 + t...  224 us
    pallas_call x1, Pallas kernels, publish(): pl.pallas_call(kernel, out_shape=tuple((shape_of(a.shape, a.dtype) for a...  7.12 us

profile of v3, /device:TPU:0, one launch (start us, length us, event | category | flops | bytes accessed | tf_op | source)
XLA Modules:
  0.0 232.3 jit_solution(17848657243055210861)
XLA Ops:
  0.7 224.3 %shard_map.236 = (bf16[1024,1024]{1,0:T(8,128)(2,1)}, bf16[1024,1024]{1,0:T(8,128)(2,1)}, f32[256,256]{1,0:T(8,128)}, f32[64,256]{1,0:T(8,128)}, f32[64,256]{1,0...) custom-call(bf16[1024,1024]{1,0:T(8,128)(2,1)} %bitcast.8, ...), custom_call_target="tpu_custom_call" | custom-call | tf_op jit(solution)/shard_map/pallas_call | solution.py:2201
  225.0 7.1 %shard_map.237 = (bf16[1024,1024]{1,0:T(8,128)(2,1)}, bf16[1024,1024]{1,0:T(8,128)(2,1)}, f32[256,256]{1,0:T(8,128)}, f32[64,256]{1,0:T(8,128)}, f32[64,256]{1,0...) custom-call(bf16[1024,1024]{1,0:T(8,128)(2,1)} %get-tuple-element.39, ...), custom_call_target="tpu_custom_call" | custom-call | tf_op jit(solution)/shard_map/pallas_call | solution.py:1454

commit v4 on v3

--- a/solution.py
+++ b/solution.py
@@ -188,8 +188,9 @@
 
 
 class LineGather:
-    def __init__(self, n, chunk, src, dst, recv, sent, own, hop=1):
+    def __init__(self, n, chunk, src, dst, recv, sent, own, hop=1, order=None):
         self.n, self.chunk, self.src, self.dst, self.hop = n, chunk, src, dst, hop
+        self.order = order or (lambda at: at)
         self.width = src.shape[1]
         self.count = src.shape[0] // chunk
         self.recv, self.sent, self.own = recv, sent, own
@@ -201,9 +202,11 @@
     def columns(self, tp):
         return pl.ds(pl.multiple_of(tp * self.width, self.width), self.width)
 
+    def rows(self, at):
+        return pl.ds(pl.multiple_of(self.order(at) * self.chunk, self.chunk), self.chunk)
+
     def place(self, tp, at):
-        rows = pl.ds(pl.multiple_of(at * self.chunk, self.chunk), self.chunk)
-        return self.dst.at[rows, self.columns(tp)]
+        return self.dst.at[self.rows(at), self.columns(tp)]
 
     def begin(self):
         pltpu.make_async_copy(self.src, self.dst.at[:, self.columns(self.me)], self.own).start()
@@ -217,7 +220,7 @@
 
         @pl.when((s >= 0) & (s < count))
         def _():
-            rows = pl.ds(pl.multiple_of(s * self.chunk, self.chunk), self.chunk)
+            rows = self.rows(s)
 
             @pl.when(me > 0)
             def _():
@@ -266,7 +269,8 @@
 
 
 class LineSum:
-    def __init__(self, n, chunk, hop, part, from_left, from_right, out, recv, sent, finish, pushed=False):
+    def __init__(self, n, chunk, hop, part, from_left, from_right, out, recv, sent, finish, pushed=False, order=None):
+        self.order = order or (lambda at: at)
         self.n, self.chunk, self.hop, self.pushed = n, chunk, hop, pushed
         self.total_rows = part.shape[0]
         self.owners = (n // 2 - 1, n // 2)
@@ -283,7 +287,7 @@
         return lax.rem(at, self.recv.shape[2])
 
     def rows(self, slot, at):
-        return pl.ds(pl.multiple_of((at * 2 + slot) * self.chunk, self.chunk), self.chunk)
+        return pl.ds(pl.multiple_of((self.order(at) * 2 + slot) * self.chunk, self.chunk), self.chunk)
 
     def send(self, here, side, slot, at):
         held = self.from_left if side == 0 else self.from_right
@@ -1674,6 +1678,12 @@
         s_ctx=AxisSum.scratch(ctx, (8, many)),
         s_fsdp=AxisSum.scratch(fsdp, (8, many)),
     )
+    def turned(i, many=1):
+        return i + many - 2 * many * lax.rem(i // many, 2) if per == 2 else i
+
+    def turned_pieces(at):
+        return turned(at, per_block)
+
     names = list(scratch)
     shapes = list(scratch.values())
     places = {}
@@ -1754,7 +1764,7 @@
             def _():
                 pass_on(i).start()
 
-        loop(0, pieces, first_norm)
+        loop(0, pieces, lambda i: first_norm(turned(i)))
         if n > 2:
             wline.relay([2])
         spread.relay([2, 3, 4])
@@ -1779,7 +1789,6 @@
             cols[at, SEGMENT : SEGMENT + 1] = ids[:, 0:1]
             final = segk[ctx - 1, q : q + 1, tok_dev - 1 : tok_dev].astype(F32)
             cols[at, VALID : VALID + 1] = jnp.where(ids[:, 0:1] != final, 1.0, 0.0)
-        half.relay([0, 1])
 
         def theirs(i):
             @pl.when(x - 1 >= 0)
@@ -1793,9 +1802,10 @@
             project(own_shard - 1, i)
 
         att, gathered = r.att, r.gathered
-        line = LineGather(n, piece, att, gathered, *g.gather, hop=reach)
-
-        def query_tile(i):
+        line = LineGather(n, piece, att, gathered, *g.gather, hop=reach, order=turned_pieces)
+
+        def query_tile(turn):
+            i = turned(turn)
             seq = i // per
             q_tile = own_shard * per + lax.rem(i, per)
             at = pl.ds(pl.multiple_of(i * TILE, TILE), TILE)
@@ -1817,26 +1827,27 @@
                 prob = (weight * (1.0 / total)).astype(BF16)
                 accum = accum + jnp.dot(prob, head_only(r.values[near, :], h), preferred_element_type=F32)
                 cols[at, LSE + h : LSE + h + 1] = top + jnp.log(total)
-                line.step((i - 1) * per_block + h * per_block // heads)
+                line.step((turn - 1) * per_block + h * per_block // heads)
             att[at, :] = accum.astype(BF16)
 
-        def sequence_forward(seq):
-            loop(seq * per_seq, seq * per_seq + per_seq, theirs)
-
-            @pl.when(seq == 0)
+        def tile_forward(i):
+            theirs(turned(i))
+            query_tile(i)
+
+            @pl.when(i == 0)
             def _():
                 if n > 3:
                     wline.relay(range(3, n))
                 wline.finish()
                 half.start([3])
 
-            loop(seq * per, seq * per + per, query_tile)
-
-            @pl.when(seq == 0)
-            def _():
-                half.relay([2, 3])
-
-        loop(0, seq_dev, sequence_forward)
+            for turn, which in enumerate(([0, 1], [2], [3])):
+
+                @pl.when(i == turn)
+                def _(which=which):
+                    half.relay(which)
+
+        loop(0, q_tiles, tile_forward)
         s1 = (q_tiles - 1) * per_block
         line.begin()
         half.cross([0, 1, 2, 3])
@@ -1875,9 +1886,9 @@
             mean = jnp.mean(scaled * unit, axis=-1, keepdims=True)
             return (r.branch[at, :].astype(F32) + r1 * (scaled - unit * mean)).astype(BF16)
 
-        two = LineSum(n, strip, hop, p_two, r.left, r.right, r.branch, *g.two, second_back, pushed=True)
-        feed = LineSum(n, strip, hop, p_feed, gathered, r.wo, xn, *g.feed, forward)
-        one = LineSum(n, strip, hop, cot, r.left, r.right, p_two, *g.two, first_back)
+        two = LineSum(n, strip, hop, p_two, r.left, r.right, r.branch, *g.two, second_back, pushed=True, order=turned_pieces)
+        feed = LineSum(n, strip, hop, p_feed, gathered, r.wo, xn, *g.feed, forward, order=turned_pieces)
+        one = LineSum(n, strip, hop, cot, r.left, r.right, p_two, *g.two, first_back, order=turned_pieces)
         parts = [wg, wu, wd]
         gffn = GradSum(fsdp, ctx, parts, [1, 1, 1], None,
                        [g.held[3 * a : 3 * a + 3] for a in range(3)], *g.gffn)
@@ -1886,7 +1897,7 @@
                        [g.held[3 * a : 3 * a + 3] for a in range(3, 8)], *g.gatt)
 
         def block_of_rows(b):
-            at = pl.ds(pl.multiple_of(b * TILE, TILE), TILE)
+            at = pl.ds(pl.multiple_of(turned(b) * TILE, TILE), TILE)
             seq = b * TILE // tok_dev
 
             def steps(j):

time: 233 us -> 232 us (level)
  no operation moved by 1% of the time
where the time goes in v4:
time: 232 us
  Pallas kernels  231 us (100%)
    pallas_call x1, Pallas kernels, layer(): pl.pallas_call(kernel, out_shape=(shape_of((rows, width), BF16),) * 2 + t...  224 us
    pallas_call x1, Pallas kernels, publish(): pl.pallas_call(kernel, out_shape=tuple((shape_of(a.shape, a.dtype) for a...  7.12 us

profile of v4, /device:TPU:0, one launch (start us, length us, event | category | flops | bytes accessed | tf_op | source)
XLA Modules:
  0.0 232.1 jit_solution(9434712941316474567)
XLA Ops:
  0.7 224.1 %shard_map.236 = (bf16[1024,1024]{1,0:T(8,128)(2,1)}, bf16[1024,1024]{1,0:T(8,128)(2,1)}, f32[256,256]{1,0:T(8,128)}, f32[64,256]{1,0:T(8,128)}, f32[64,256]{1,0...) custom-call(bf16[1024,1024]{1,0:T(8,128)(2,1)} %bitcast.8, ...), custom_call_target="tpu_custom_call" | custom-call | tf_op jit(solution)/shard_map/pallas_call | solution.py:2212
  224.7 7.1 %shard_map.237 = (bf16[1024,1024]{1,0:T(8,128)(2,1)}, bf16[1024,1024]{1,0:T(8,128)(2,1)}, f32[256,256]{1,0:T(8,128)}, f32[64,256]{1,0:T(8,128)}, f32[64,256]{1,0...) custom-call(bf16[1024,1024]{1,0:T(8,128)(2,1)} %get-tuple-element.39, ...), custom_call_target="tpu_custom_call" | custom-call | tf_op jit(solution)/shard_map/pallas_call | solution.py:1458

commit v5 on v3

--- a/solution.py
+++ b/solution.py
@@ -198,6 +198,13 @@
     def steps(self):
         return self.count + self.hop * (self.n - 1)
 
+    def flag(self, tp, at):
+        shape = self.recv.shape
+        if len(shape) == 2:
+            return self.recv.at[tp, at]
+        i = tp * self.count + at
+        return self.recv.at[i // (shape[1] * shape[2]), i // shape[2] % shape[1], i % shape[2]]
+
     def columns(self, tp):
         return pl.ds(pl.multiple_of(tp * self.width, self.width), self.width)
 
@@ -221,11 +228,11 @@
 
             @pl.when(me > 0)
             def _():
-                remote(self.src.at[rows], self.place(me, s), self.sent.at[0], self.recv.at[me, s], left).start()
+                remote(self.src.at[rows], self.place(me, s), self.sent.at[0], self.flag(me, s), left).start()
 
             @pl.when(me < n - 1)
             def _():
-                remote(self.src.at[rows], self.place(me, s), self.sent.at[1], self.recv.at[me, s], right).start()
+                remote(self.src.at[rows], self.place(me, s), self.sent.at[1], self.flag(me, s), right).start()
 
         for away in range(1, n):
             at = s - away * self.hop
@@ -235,26 +242,26 @@
                 @pl.when((tp >= 0) & (tp < n) & (at >= 0) & (at < count))
                 def _(tp=tp, onward=onward, sign=sign, at=at):
                     here = self.place(tp, at)
-                    wait_came(here, self.sent.at[2], self.recv.at[tp, at])
+                    wait_came(here, self.sent.at[2], self.flag(tp, at))
 
                     @pl.when((me < n - 1) if sign < 0 else (me > 0))
                     def _():
-                        remote(here, here, self.sent.at[2], self.recv.at[tp, at], onward).start()
+                        remote(here, here, self.sent.at[2], self.flag(tp, at), onward).start()
 
     def drain(self):
         n, me = self.n, self.me
 
         @pl.when(me > 0)
         def _():
-            wait_sent(self.src, self.sent.at[0], self.recv.at[0, 0])
+            wait_sent(self.src, self.sent.at[0], self.flag(0, 0))
 
         @pl.when(me < n - 1)
         def _():
-            wait_sent(self.src, self.sent.at[1], self.recv.at[0, 0])
+            wait_sent(self.src, self.sent.at[1], self.flag(0, 0))
 
         @pl.when((me > 0) & (me < n - 1))
         def _():
-            wait_sent(self.dst.at[:, pl.ds(0, (n - 1) * self.width)], self.sent.at[2], self.recv.at[0, 0])
+            wait_sent(self.dst.at[:, pl.ds(0, (n - 1) * self.width)], self.sent.at[2], self.flag(0, 0))
 
     @staticmethod
     def scratch(n, count):
@@ -1663,7 +1670,7 @@
         half=HalfSpread.scratch(fsdp, 4),
         share=CtxShare.scratch(ctx),
         wline=RowGather.scratch(n),
-        gather=LineGather.scratch(n, rows // piece),
+        gather=LineGather.scratch(n, rows // piece)[1:],
         two=LineSum.scratch(n, rows, width, strip)[2:],
         feed=LineSum.scratch(n, rows, width, strip)[2:],
         gffn=GradSum.semaphores(fsdp, ctx, 3),
@@ -1793,7 +1800,7 @@
             project(own_shard - 1, i)
 
         att, gathered = r.att, r.gathered
-        line = LineGather(n, piece, att, gathered, *g.gather, hop=reach)
+        line = LineGather(n, piece, att, gathered, g.feed[0], *g.gather, hop=reach)
 
         def query_tile(i):
             seq = i // per

time: 233 us -> 232 us (level)
  no operation moved by 1% of the time
where the time goes in v5:
time: 232 us
  Pallas kernels  231 us (100%)
    pallas_call x1, Pallas kernels, layer(): pl.pallas_call(kernel, out_shape=(shape_of((rows, width), BF16),) * 2 + t...  224 us
    pallas_call x1, Pallas kernels, publish(): pl.pallas_call(kernel, out_shape=tuple((shape_of(a.shape, a.dtype) for a...  7.12 us

profile of v5, /device:TPU:0, one launch (start us, length us, event | category | flops | bytes accessed | tf_op | source)
XLA Modules:
  0.0 231.6 jit_solution(12592716745750344237)
XLA Ops:
  0.7 223.7 %shard_map.236 = (bf16[1024,1024]{1,0:T(8,128)(2,1)}, bf16[1024,1024]{1,0:T(8,128)(2,1)}, f32[256,256]{1,0:T(8,128)}, f32[64,256]{1,0:T(8,128)}, f32[64,256]{1,0...) custom-call(bf16[1024,1024]{1,0:T(8,128)(2,1)} %bitcast.8, ...), custom_call_target="tpu_custom_call" | custom-call | tf_op jit(solution)/shard_map/pallas_call | solution.py:2208
  224.3 7.1 %shard_map.237 = (bf16[1024,1024]{1,0:T(8,128)(2,1)}, bf16[1024,1024]{1,0:T(8,128)(2,1)}, f32[256,256]{1,0:T(8,128)}, f32[64,256]{1,0:T(8,128)}, f32[64,256]{1,0...) custom-call(bf16[1024,1024]{1,0:T(8,128)(2,1)} %get-tuple-element.39, ...), custom_call_target="tpu_custom_call" | custom-call | tf_op jit(solution)/shard_map/pallas_call | solution.py:1461
